TPU v7x, 32 devices: a whole 2x2x4 slice. The times are simulated.
32 devices in a mesh: row: 4 (over y, x), col: 4 (over z), layer: 2 (over core).
Axes of the slice: x: 2, y: 2, z: 4, core: 2. Of those that a mesh axis runs over, the one named last changes fastest.
Arguments:
- a_blocks: bfloat16 [4, 4, 2, 24, 128, 128], P('row', 'col', 'layer'), may hold values from -6 to 6
- a_cells: int32 [4, 4, 2, 24], P('row', 'col', 'layer'), may hold values from 0 to 31, as said below
- a_count: int32 [4, 4, 2], P('row', 'col', 'layer'), may hold values from 12 to 24, as said below
- b_blocks: bfloat16 [4, 4, 2, 80, 128, 128], P('row', 'col', 'layer'), may hold values from -0.125 to 0.125
- b_cells: int32 [4, 4, 2, 80], P('row', 'col', 'layer'), may hold values from 0 to 127, as said below
- b_count: int32 [4, 4, 2], P('row', 'col', 'layer'), may hold values from 40 to 80, as said below
- c_cells: int32 [4, 4, 32], P('row', 'col'), may hold values from 0 to 63, as said below
Outputs:
- c_blocks: float32 [4, 4, 32, 128, 128], P('row', 'col', 'layer')
Inputs may be any that keep to these rules, and one draw needn't show every extreme that they name: `a_cells`: positions are distinct within each A panel. `a_count`: some panel is full in every draw. `b_cells`: positions are distinct within each B panel. `b_count`: some panel is full in every draw. `c_cells`: positions are distinct within each tile.
All inputs are finite; a program needn't handle non-finite values.
Results may differ from a plain program's by a relative error of at most 0.0003.
Values may be sent and summed in bfloat16 or wider, within the bound.
No kernel may reach another device: no remote copies, remote signals or barrier semaphores. Data moves between devices by JAX's collectives and lax.ppermute only.
A program may use at most 128 MiB of HBM per device.

v0:
```python
import jax
import jax.numpy as jnp
from jax import lax
from jax.sharding import PartitionSpec as P

CR = 4
CC = 16
KW = 8


def shifted(value, axis, by):
    size = lax.axis_size(axis)
    return lax.ppermute(value, axis, [(i, (i + by) % size) for i in range(size)])


def densify(blocks, cell_list, live_count, height, breadth):
    capacity = cell_list.shape[0]
    slot_ids = jnp.arange(capacity, dtype=jnp.int32)
    positions = jnp.arange(height * breadth, dtype=jnp.int32)
    matches = (cell_list[None, :] == positions[:, None]) & (slot_ids[None, :] < live_count)
    slot_index = jnp.sum(jnp.where(matches, slot_ids[None, :], 0), axis=1)
    present = jnp.any(matches, axis=1)
    picked = jnp.take(blocks, slot_index, axis=0)
    picked = jnp.where(present[:, None, None], picked, jnp.zeros((), blocks.dtype))
    return picked.reshape(height, breadth, blocks.shape[1], blocks.shape[2])


def kept_product(left, right, kept_rows, kept_cols):
    left_rows = jnp.take(left, kept_rows, axis=0)
    right_cols = jnp.take(right, kept_cols, axis=1)
    return jnp.einsum("tkxz,ktzy->txy", left_rows, right_cols, preferred_element_type=jnp.float32)


def on_device(a_blocks, a_cells, a_count, b_blocks, b_cells, b_count, c_cells):
    own_left = densify(a_blocks[0, 0, 0], a_cells[0, 0, 0], a_count[0, 0, 0], CR, KW)
    own_right = densify(b_blocks[0, 0, 0], b_cells[0, 0, 0], b_count[0, 0, 0], KW, CC)
    moved_blocks, moved_cells, moved_count = shifted((a_blocks, a_cells, a_count), "row", -1)
    next_left = densify(moved_blocks[0, 0, 0], moved_cells[0, 0, 0], moved_count[0, 0, 0], CR, KW)
    shifted_blocks, shifted_cells, shifted_count = shifted((b_blocks, b_cells, b_count), "col", -1)
    next_right = densify(
        shifted_blocks[0, 0, 0], shifted_cells[0, 0, 0], shifted_count[0, 0, 0], KW, CC
    )
    slot_list = c_cells[0, 0]
    kept_rows = slot_list // CC
    kept_cols = slot_list % CC
    first_stop = kept_product(own_left, own_right, kept_rows, kept_cols)
    both_stops = first_stop + kept_product(next_left, next_right, kept_rows, kept_cols)
    summed = lax.psum_scatter(both_stops, "layer", scatter_dimension=0, tiled=True)
    return summed[None, None]


def solution(mesh):
    return jax.shard_map(
        on_device,
        mesh=mesh,
        in_specs=(
            P("row", "col", "layer", None, None, None),
            P("row", "col", "layer", None),
            P("row", "col", "layer"),
            P("row", "col", "layer", None, None, None),
            P("row", "col", "layer", None),
            P("row", "col", "layer"),
            P("row", "col", None),
        ),
        out_specs=P("row", "col", "layer", None, None),
        check_vma=False,
    )
```

profile of v0, /device:TPU:0, one launch (start us, length us, event | category | flops | bytes accessed | tf_op | source)
XLA Modules:
  0.0 121.2 jit_solution(2757350563822940580)
XLA Ops:
  6.5 0.0 reduce-scatter.2.cloned.1.call-start
  6.5 5.1 %collective-permute-start.4 = (s32[1,1,1]{2,1,0:T(1,128)}, s32[1,1,1]{2,1,0:T(1,128)}, u32[]{:S(2)}, u32[]{:S(2)}) collective-permute-start(s32[1,1,1]{2,1,0:T(1,128)} %param.20), channel_id=1, source_target_pairs={{0,6},{2,0},{4,2},{6,4},{1,7},{3,1},{5,3},{7,5},{8,14},{10,8},{12,... | collective-permute-start | bytes 20 | tf_op jit(solution)/shard_map/ppermute | solution.py:13
  11.6 0.4 collective-permute-start.3
  12.1 0.4 collective-permute-start.5
  12.5 2.4 %collective-permute-start.1 = (s32[1,1,1]{2,1,0:T(1,128)}, s32[1,1,1]{2,1,0:T(1,128)}, u32[]{:S(2)}, u32[]{:S(2)}) collective-permute-start(s32[1,1,1]{2,1,0:T(1,128)} %param.17), channel_id=1, source_target_pairs={{0,24},{8,0},{16,8},{24,16},{1,25},{9,1},{17,9},{25,17},{2,26},{10... | collective-permute-start | bytes 20 | tf_op jit(solution)/shard_map/ppermute | solution.py:13
  15.0 0.5 collective-permute-start
  16.2 0.8 select_reduce_fusion.1
  16.9 0.8 fusion.19
  18.4 0.7 select_reduce_fusion.3
  19.1 0.7 fusion.23
  19.9 0.7 compare_and_fusion.4
  20.6 4.8 %gather_fusion.2 = bf16[128,128,128]{2,1,0:T(8,128)(2,1)} fusion(bf16[80,128,128]{2,1,0:T(8,128)(2,1)} %bitcast.56, s32[1024]{0:T(1024)S(1)} %pad_clamp_fusion.3), kind=kCustom, calls=%fused_computation.2.clone | custom fusion | bytes 8389120 | tf_op jit(solution)/shard_map/jit(_take)/gather | solution.py:23
  25.4 4.0 %select_select_fusion.1 = bf16[128,128,128]{2,1,0:T(8,128)(2,1)} fusion(bf16[128,128,128]{2,1,0:T(8,128)(2,1)} %gather_fusion.2, pred[128]{0:T(512)(128)(4,1)S(1)} %compare_and_fusion.3, pred[128]{0:T(512)(128)(4,1)S(1)} %fusion.19), kind=kLoop, calls=%fused_computation.21 | loop fusion | flops 4194304 | bytes 8388864 | tf_op jit(solution)/shard_map/jit(_where)/select_n | solution.py:24
  29.4 0.0 copy-start
  29.4 7.3 %gather_fusion.3 = bf16[32,8,128,128]{3,2,1,0:T(8,128)(2,1)} fusion(bf16[8,16,128,128]{3,2,1,0:T(8,128)(2,1)} %bitcast.54, s32[1024]{0:T(1024)S(1)} %get-tuple-element.15), kind=kCustom, calls=%fused_computation.3.clone | custom fusion | bytes 16777344 | tf_op jit(solution)/shard_map/jit(_take)/gather | solution.py:30
  36.7 0.0 copy-done
  36.7 0.7 gather_fusion
  37.5 0.2 select_select_fusion.3
  37.7 5.0 %gather_fusion.1 = bf16[32,8,128,128]{3,2,1,0:T(8,128)(2,1)} fusion(bf16[4,8,128,128]{3,2,1,0:T(8,128)(2,1)S(1)} %bitcast.52, s32[1024]{0:T(1024)S(1)} %get-tuple-element.16), kind=kCustom, calls=%fused_computation.1.clone | custom fusion | bytes 16777344 | tf_op jit(solution)/shard_map/jit(_take)/gather | solution.py:29
  42.6 0.0 collective-permute-done.4
  42.6 1.4 %collective-permute-start.2 = (bf16[1,1,1,24,128,128]{5,4,3,2,1,0:T(8,128)(2,1)S(1)}, bf16[1,1,1,24,128,128]{5,4,3,2,1,0:T(8,128)(2,1)S(1)}, u32[]{:S(2)}, u32[]{:S(2)}) collective-permute-start(bf16[1,1,1,24,128,128]{5,4,3,2,1,0:T(8,128)(2,1)S(1)} %copy-done), channel_id=1, source_target_pairs={{0,24},{8,0},{16,8},{24,16},{1,25},{9,1},{17,9},{25,17},{2,26},{10... | collective-permute-start | bytes 2359304 | tf_op jit(solution)/shard_map/ppermute | solution.py:13
  44.1 0.6 iota_compare_fusion.4
  44.6 0.0 collective-permute-done.1
  44.6 0.7 iota_compare_fusion.5
  45.3 0.0 collective-permute-done
  45.3 0.1 select_reduce_fusion.2
  45.4 0.1 fusion.25
  45.6 0.0 collective-permute-done.3
  45.6 0.1 select_reduce_fusion
  45.7 0.1 fusion.21
  45.8 14.7 %collective-permute-done.2 = bf16[1,1,1,24,128,128]{5,4,3,2,1,0:T(8,128)(2,1)S(1)} collective-permute-done((bf16[1,1,1,24,128,128]{5,4,3,2,1,0:T(8,128)(2,1)S(1)}, bf16[1,1,1,24,128,128]{5,4,3,2,1,0:T(8,128)(2,1)S(1)}, u32[]{:S(2)}, u32[]{:S(2)}) %collective-permute-start.2) | collective-permute-done | bytes 786464 | tf_op jit(solution)/shard_map/ppermute | solution.py:13
  60.5 0.7 gather_fusion.4
  61.3 0.2 select_select_fusion.2
  61.5 5.0 %gather_fusion.5 = bf16[32,8,128,128]{3,2,1,0:T(8,128)(2,1)} fusion(bf16[4,8,128,128]{3,2,1,0:T(8,128)(2,1)S(1)} %bitcast.53, s32[1024]{0:T(1024)S(1)} %get-tuple-element.16), kind=kCustom, calls=%fused_computation.5.clone | custom fusion | bytes 16777344 | tf_op jit(solution)/shard_map/jit(_take)/gather | solution.py:29
  66.5 4.0 %collective-permute-done.5 = bf16[1,1,1,80,128,128]{5,4,3,2,1,0:T(8,128)(2,1)} collective-permute-done((bf16[1,1,1,80,128,128]{5,4,3,2,1,0:T(8,128)(2,1)}, bf16[1,1,1,80,128,128]{5,4,3,2,1,0:T(8,128)(2,1)}, u32[]{:S(2)}, u32[]{:S(2)}) %collective-permute-start.5) | collective-permute-done | bytes 2621472 | tf_op jit(solution)/shard_map/ppermute | solution.py:13
  70.4 4.9 %gather_fusion.6 = bf16[128,128,128]{2,1,0:T(8,128)(2,1)} fusion(bf16[80,128,128]{2,1,0:T(8,128)(2,1)} %bitcast.18, s32[1024]{0:T(1024)S(1)} %pad_clamp_fusion), kind=kCustom, calls=%fused_computation.6.clone | custom fusion | bytes 8389120 | tf_op jit(solution)/shard_map/jit(_take)/gather | solution.py:23
  75.3 4.1 %select_select_fusion = bf16[128,128,128]{2,1,0:T(8,128)(2,1)} fusion(bf16[128,128,128]{2,1,0:T(8,128)(2,1)} %gather_fusion.6, pred[128]{0:T(512)(128)(4,1)S(1)} %compare_and_fusion, pred[128]{0:T(512)(128)(4,1)S(1)} %fusion.21), kind=kLoop, calls=%fused_computation.20 | loop fusion | flops 4194304 | bytes 8388864 | tf_op jit(solution)/shard_map/jit(_where)/select_n | solution.py:24
  79.4 7.2 %gather_fusion.7 = bf16[32,8,128,128]{3,2,1,0:T(8,128)(2,1)} fusion(bf16[8,16,128,128]{3,2,1,0:T(8,128)(2,1)} %bitcast.55, s32[1024]{0:T(1024)S(1)} %get-tuple-element.15), kind=kCustom, calls=%fused_computation.7.clone | custom fusion | bytes 16777344 | tf_op jit(solution)/shard_map/jit(_take)/gather | solution.py:30
  86.6 8.3 %fusion = f32[32,128,128,1]{2,1,3,0:T(8,128)S(1)} fusion(bf16[32,8,128,128]{3,2,1,0:T(8,128)(2,1)} %gather_fusion.7, bf16[32,8,128,128]{3,2,1,0:T(8,128)(2,1)} %gather_fusion.5, pred[32]{0:T(512)(128)(4,1)S(1)} %get-tuple-element.13, pred[32]{0:T(512)(128)(4,1)S(1)} %get-tuple-element.6), kind=kOutput, calls=%fused_computation.8 | convolution fusion | flops 1082130432 | bytes 18874432 | tf_op jit(solution)/shard_map/tkxz,ktzy->txy/dot_general | solution.py:31
  94.9 9.7 %bitcast_add_fusion = f32[32,128,128]{2,1,0:T(8,128)} fusion(f32[32,128,128,1]{2,1,3,0:T(8,128)S(1)} %fusion, bf16[32,8,128,128]{3,2,1,0:T(8,128)(2,1)} %gather_fusion.3, pred[32]{0:T(512)(128)(4,1)S(1)} %get-tuple-element.13, bf16[32,8,128,128]{3,2,1,0:T(8,128)(2,1)} %gather_fusion.1, pred[32]{0:T(512)(128)(4,1)S(1)} %get-tuple-element.6), kind=kOutput, calls=%fused_computation.24 | convolution fusion | flops 1082654720 | bytes 20971584 | tf_op jit(solution)/shard_map/tkxz,ktzy->txy/dot_general | solution.py:31
  104.5 0.0 reduce-scatter.2.cloned.1.call-update
  104.5 9.8 %reduce-scatter.2.cloned.1.call-done = f32[16,128,128]{2,1,0:T(8,128)} async-done(((f32[32,128,128]{2,1,0:T(8,128)}), f32[16,128,128]{2,1,0:T(8,128)}) %reduce-scatter.2.cloned.1.call-update) | async-done | bytes 1048592 | tf_op jit(solution)/shard_map/reduce_scatter | solution.py:48
  (15 shorter events, 0.1 us)
Async XLA Ops:
  6.5 107.8 %reduce-scatter.2.cloned.1.call-start = ((), (), s32[]{:S(2)}) async-start(), calls=%async_computation.1 | async-start | bytes 3145728 | tf_op jit(solution)/shard_map/reduce_scatter | solution.py:48
  6.5 36.1 %collective-permute-start.4 = (s32[1,1,1]{2,1,0:T(1,128)}, s32[1,1,1]{2,1,0:T(1,128)}, u32[]{:S(2)}, u32[]{:S(2)}) collective-permute-start(s32[1,1,1]{2,1,0:T(1,128)} %param.20), channel_id=1, source_target_pairs={{0,6},{2,0},{4,2},{6,4},{1,7},{3,1},{5,3},{7,5},{8,14},{10,8},{12,... | collective-permute-start | bytes 20 | tf_op jit(solution)/shard_map/ppermute | solution.py:13
  11.6 34.0 %collective-permute-start.3 = (s32[1,1,1,80]{3,2,1,0:T(1,128)}, s32[1,1,1,80]{3,2,1,0:T(1,128)S(1)}, u32[]{:S(2)}, u32[]{:S(2)}) collective-permute-start(s32[1,1,1,80]{3,2,1,0:T(1,128)} %param.19), channel_id=1, source_target_pairs={{0,6},{2,0},{4,2},{6,4},{1,7},{3,1},{5,3},{7,5},{8,14},{10,8},{12,... | collective-permute-start | bytes 968 | tf_op jit(solution)/shard_map/ppermute | solution.py:13
  12.1 58.4 %collective-permute-start.5 = (bf16[1,1,1,80,128,128]{5,4,3,2,1,0:T(8,128)(2,1)}, bf16[1,1,1,80,128,128]{5,4,3,2,1,0:T(8,128)(2,1)}, u32[]{:S(2)}, u32[]{:S(2)}) collective-permute-start(bf16[1,1,1,80,128,128]{5,4,3,2,1,0:T(8,128)(2,1)} %param.18), channel_id=1, source_target_pairs={{0,6},{2,0},{4,2},{6,4},{1,7},{3,1},{5,3},{7,5},{8,14},{10,8},{12,... | collective-permute-start | bytes 7864328 | tf_op jit(solution)/shard_map/ppermute | solution.py:13
  12.5 32.1 %collective-permute-start.1 = (s32[1,1,1]{2,1,0:T(1,128)}, s32[1,1,1]{2,1,0:T(1,128)}, u32[]{:S(2)}, u32[]{:S(2)}) collective-permute-start(s32[1,1,1]{2,1,0:T(1,128)} %param.17), channel_id=1, source_target_pairs={{0,24},{8,0},{16,8},{24,16},{1,25},{9,1},{17,9},{25,17},{2,26},{10... | collective-permute-start | bytes 20 | tf_op jit(solution)/shard_map/ppermute | solution.py:13
  15.0 30.4 %collective-permute-start = (s32[1,1,1,24]{3,2,1,0:T(1,128)}, s32[1,1,1,24]{3,2,1,0:T(1,128)S(1)}, u32[]{:S(2)}, u32[]{:S(2)}) collective-permute-start(s32[1,1,1,24]{3,2,1,0:T(1,128)} %param.16), channel_id=1, source_target_pairs={{0,24},{8,0},{16,8},{24,16},{1,25},{9,1},{17,9},{25,17},{2,26},{10... | collective-permute-start | bytes 296 | tf_op jit(solution)/shard_map/ppermute | solution.py:13
  29.4 7.3 %copy-start = (bf16[1,1,1,24,128,128]{5,4,3,2,1,0:T(8,128)(2,1)S(1)}, bf16[1,1,1,24,128,128]{5,4,3,2,1,0:T(8,128)(2,1)}, u32[]{:S(2)}) copy-start(bf16[1,1,1,24,128,128]{5,4,3,2,1,0:T(8,128)(2,1)} %param.15) | copy-start | bytes 2359300
  42.6 17.9 %collective-permute-start.2 = (bf16[1,1,1,24,128,128]{5,4,3,2,1,0:T(8,128)(2,1)S(1)}, bf16[1,1,1,24,128,128]{5,4,3,2,1,0:T(8,128)(2,1)S(1)}, u32[]{:S(2)}, u32[]{:S(2)}) collective-permute-start(bf16[1,1,1,24,128,128]{5,4,3,2,1,0:T(8,128)(2,1)S(1)} %copy-done), channel_id=1, source_target_pairs={{0,24},{8,0},{16,8},{24,16},{1,25},{9,1},{17,9},{25,17},{2,26},{10... | collective-permute-start | bytes 2359304 | tf_op jit(solution)/shard_map/ppermute | solution.py:13
Sparse Core Ops, SparseCore 0:
  104.7 9.6 reduce-scatter.1
where the time goes:
time: 122 us; the launch traced here: 121 us
  local copies, waits for them, and re-layouts  35.5 us (29%)
  waiting for transfers between devices  28.5 us (23%)
  matrix products  17.9 us (15%)
  between operations  14.9 us (12%)
  other arithmetic  14 us (11%)
  starting transfers between devices  10.4 us (9%)
    ppermute x6, waiting for transfers between devices, shifted(): lax.ppermute(value, axis, [(i, (i + by) % size) for i in range(size)])  18.7 us
    dot_general x2, matrix products, kept_product(): jnp.einsum('tkxz,ktzy->txy', left_rows, right_cols, preferred_element_typ...  17.9 us
    gather x2, local copies, waits for them, and re-layouts, kept_product(): right_cols = jnp.take(right, kept_cols, axis=1)  14.4 us
    gather x4, local copies, waits for them, and re-layouts, densify(): picked = jnp.take(blocks, slot_index, axis=0)  11.2 us
    ppermute x6, starting transfers between devices, shifted(): lax.ppermute(value, axis, [(i, (i + by) % size) for i in range(size)])  10.4 us
    gather x2, local copies, waits for them, and re-layouts, kept_product(): left_rows = jnp.take(left, kept_rows, axis=0)  9.92 us
    reduce_scatter x1, waiting for transfers between devices, on_device(): lax.psum_scatter(both_stops, 'layer', scatter_dimension=0, tiled=True)  9.83 us
    select_n x4, other arithmetic, densify(): jnp.where(present[:, None, None], picked, jnp.zeros((), blocks.dtype))  8.57 us
  transfers between devices with their start and end apart: 7, of which 3 were waited for; matrix products, arithmetic and copies ran while one was open for 28% of the time, Pallas kernels for 0%

commit v1 on v0

v1 whole, which is shorter than its diff:
```python
import functools

import jax
import jax.numpy as jnp
from jax import lax
from jax.experimental import pallas as pl
from jax.experimental.pallas import tpu as pltpu
from jax.sharding import PartitionSpec as P

CR = 4
CC = 16
KW = 8
PAIR = 2
GROUPS = CC // PAIR

ANY = pl.BlockSpec(memory_space=pl.ANY)
SMEM = pl.BlockSpec(memory_space=pltpu.SMEM)


def slot_of_cell(cell_list, live_count, cells):
    slot_ids = jnp.arange(cell_list.shape[0], dtype=jnp.int32)
    positions = jnp.arange(cells, dtype=jnp.int32)
    matches = (cell_list[None, :] == positions[:, None]) & (slot_ids[None, :] < live_count)
    return jnp.sum(jnp.where(matches, slot_ids[None, :] + 1, 0), axis=1) - 1


def fill_cell(slot, blocks, target, sem):
    @pl.when(slot >= 0)
    def _():
        pltpu.make_async_copy(blocks.at[slot], target, sem).start()

    @pl.when(slot < 0)
    def _():
        target[...] = jnp.zeros(target.shape, target.dtype)


def wait_cell(slot, blocks, target, sem):
    @pl.when(slot >= 0)
    def _():
        pltpu.make_async_copy(blocks.at[slot], target, sem).wait()


def left_cell(left, cell, bs):
    return left.at[pl.ds((cell // KW) * bs, bs), pl.ds((cell % KW) * bs, bs)]


def right_cell(right, inner, col, bs):
    start = pl.multiple_of((col % PAIR) * bs, bs)
    return right.at[col // PAIR, pl.ds(inner * bs, bs), pl.ds(start, bs)]


def kept_blocks(kept, rot, acc, outs, out_sem):
    total = sum(out.shape[0] for out in outs)
    copies = []
    for place in range(total):
        cell = kept[lax.rem(place + rot[0], total)]
        out = outs[place // outs[0].shape[0]]
        copies.append(
            pltpu.make_async_copy(
                acc.at[cell % CC, cell // CC], out.at[place % out.shape[0]], out_sem.at[place]
            )
        )
    for copy in copies:
        copy.start()
    for copy in copies:
        copy.wait()


def multiply(left, right, acc, group, bs):
    product = jnp.dot(left[...], right[group], preferred_element_type=jnp.float32)
    for half in range(PAIR):
        for row in range(CR):
            acc[group * PAIR + half, row] = product[
                row * bs : (row + 1) * bs, half * bs : (half + 1) * bs
            ]


def first_kernel(bs, layers, a_slot, b_slot, kept, rot, a_blocks, b_blocks, *refs):
    outs, dense = refs[:layers], refs[layers]
    left, right, acc, a_sem, b_sem, out_sem, dense_sem = refs[layers + 1 :]

    for cell in range(CR * KW):
        fill_cell(a_slot[cell], a_blocks, left_cell(left, cell, bs), a_sem.at[cell])

    @pl.loop(0, CC)
    def _(col):
        for inner in range(KW):
            fill_cell(
                b_slot[inner * CC + col],
                b_blocks,
                right_cell(right, inner, col, bs),
                b_sem.at[inner * CC + col],
            )

    for cell in range(CR * KW):
        wait_cell(a_slot[cell], a_blocks, left_cell(left, cell, bs), a_sem.at[cell])

    @pl.loop(0, GROUPS)
    def _(group):
        for half in range(PAIR):
            col = group * PAIR + half
            for inner in range(KW):
                wait_cell(
                    b_slot[inner * CC + col],
                    b_blocks,
                    right_cell(right, inner, col, bs),
                    b_sem.at[inner * CC + col],
                )
        multiply(left, right, acc, group, bs)

    dense_copy = pltpu.make_async_copy(right, dense, dense_sem)
    dense_copy.start()
    kept_blocks(kept, rot, acc, outs, out_sem)
    dense_copy.wait()


def second_kernel(bs, layers, a_slot, kept, rot, a_blocks, dense, *refs):
    outs = refs[:layers]
    left, right, acc, a_sem, dense_sem, out_sem = refs[layers:]

    for cell in range(CR * KW):
        fill_cell(a_slot[cell], a_blocks, left_cell(left, cell, bs), a_sem.at[cell])

    for group in range(GROUPS):
        pltpu.make_async_copy(dense.at[group], right.at[group], dense_sem.at[group]).start()

    for cell in range(CR * KW):
        wait_cell(a_slot[cell], a_blocks, left_cell(left, cell, bs), a_sem.at[cell])

    @pl.loop(0, GROUPS)
    def _(group):
        pltpu.make_async_copy(dense.at[group], right.at[group], dense_sem.at[group]).wait()
        multiply(left, right, acc, group, bs)

    kept_blocks(kept, rot, acc, outs, out_sem)


def run_first(layers, a_slot, b_slot, kept, rot, a_blocks, b_blocks):
    bs, capacity = a_blocks.shape[-1], kept.shape[0]
    share = jax.ShapeDtypeStruct((capacity // layers, bs, bs), jnp.float32)
    dense = jax.ShapeDtypeStruct((GROUPS, KW * bs, PAIR * bs), b_blocks.dtype)
    return pl.pallas_call(
        functools.partial(first_kernel, bs, layers),
        name="first_product",
        out_shape=[share] * layers + [dense],
        in_specs=[SMEM] * 4 + [ANY] * 2,
        out_specs=[ANY] * (layers + 1),
        scratch_shapes=[
            pltpu.VMEM((CR * bs, KW * bs), a_blocks.dtype),
            pltpu.VMEM(dense.shape, dense.dtype),
            pltpu.VMEM((CC, CR, bs, bs), jnp.float32),
            pltpu.SemaphoreType.DMA((CR * KW,)),
            pltpu.SemaphoreType.DMA((KW * CC,)),
            pltpu.SemaphoreType.DMA((capacity,)),
            pltpu.SemaphoreType.DMA,
        ],
        compiler_params=pltpu.CompilerParams(vmem_limit_bytes=24 << 20),
        cost_estimate=pl.CostEstimate(
            flops=2 * CR * KW * CC * bs**3, bytes_accessed=12 << 20, transcendentals=0
        ),
    )(a_slot, b_slot, kept, rot, a_blocks, b_blocks)


def run_second(layers, a_slot, kept, rot, a_blocks, dense):
    bs, capacity = a_blocks.shape[-1], kept.shape[0]
    share = jax.ShapeDtypeStruct((capacity // layers, bs, bs), jnp.float32)
    return pl.pallas_call(
        functools.partial(second_kernel, bs, layers),
        name="second_product",
        out_shape=[share] * layers,
        in_specs=[SMEM] * 3 + [ANY] * 2,
        out_specs=[ANY] * layers,
        scratch_shapes=[
            pltpu.VMEM((CR * bs, KW * bs), a_blocks.dtype),
            pltpu.VMEM(dense.shape, dense.dtype),
            pltpu.VMEM((CC, CR, bs, bs), jnp.float32),
            pltpu.SemaphoreType.DMA((CR * KW,)),
            pltpu.SemaphoreType.DMA((GROUPS,)),
            pltpu.SemaphoreType.DMA((capacity,)),
        ],
        compiler_params=pltpu.CompilerParams(vmem_limit_bytes=24 << 20),
        cost_estimate=pl.CostEstimate(
            flops=2 * CR * KW * CC * bs**3, bytes_accessed=8 << 20, transcendentals=0
        ),
    )(a_slot, kept, rot, a_blocks, dense)


def layer_sum(shares, layers):
    total = shares[0]
    for step in range(1, layers):
        perm = [(i, (i + step) % layers) for i in range(layers)]
        total = total + lax.ppermute(shares[step], "layer", perm)
    return total


def on_device(rows, cols, layers, a_blocks, a_cells, a_count, b_blocks, b_cells, b_count, c_cells):
    a_blocks, a_cells, a_count = a_blocks[0, 0, 0], a_cells[0, 0, 0], a_count[0, 0, 0]
    b_blocks, b_cells, b_count = b_blocks[0, 0, 0], b_cells[0, 0, 0], b_count[0, 0, 0]
    kept = c_cells[0, 0]

    to_b = [
        (((r + 1) % rows) * cols + c, r * cols + (c + 1) % cols)
        for r in range(rows)
        for c in range(cols)
    ]
    moved_blocks = lax.ppermute(a_blocks, ("row", "col"), to_b)
    a_slot = slot_of_cell(a_cells, a_count, CR * KW)
    moved_slot = lax.ppermute(a_slot, ("row", "col"), to_b)
    moved_kept = lax.ppermute(kept, "col", [(c, (c + 1) % cols) for c in range(cols)])

    b_slot = slot_of_cell(b_cells, b_count, KW * CC)
    rot = (lax.axis_index("layer") * (kept.shape[0] // layers)).astype(jnp.int32).reshape(1)
    *first, dense = run_first(layers, a_slot, b_slot, kept, rot, a_blocks, b_blocks)
    own = layer_sum(first, layers)
    moved_blocks, own = lax.optimization_barrier((moved_blocks, own))
    second = run_second(layers, moved_slot, moved_kept, rot, moved_blocks, dense)
    other = layer_sum(second, layers)
    back = lax.ppermute(other, "col", [(c, (c - 1) % cols) for c in range(cols)])
    return (own + back)[None, None]


def solution(mesh):
    sizes = mesh.shape
    return jax.shard_map(
        functools.partial(on_device, sizes["row"], sizes["col"], sizes["layer"]),
        mesh=mesh,
        in_specs=(
            P("row", "col", "layer", None, None, None),
            P("row", "col", "layer", None),
            P("row", "col", "layer"),
            P("row", "col", "layer", None, None, None),
            P("row", "col", "layer", None),
            P("row", "col", "layer"),
            P("row", "col", None),
        ),
        out_specs=P("row", "col", "layer", None, None),
        check_vma=False,
    )
```

time: 122 us -> 83.1 us (0.68)
  local copies, waits for them, and re-layouts: 35.5 us -> 3.52 us
  Pallas kernels: 0 us -> 22 us
  matrix products: 17.9 us -> 0 us
  waiting for transfers between devices: 28.5 us -> 42.8 us
  between operations: 14.9 us -> 1.38 us
  other arithmetic: 14 us -> 2.91 us
    gather x8 -> x0, local copies, waits for them, and re-layouts: 35.5 us -> none  [the longest x2 14.4 us: kept_product(): right_cols = jnp.take(right, kept_cols, axis=1)]
    ppermute x6, waiting for transfers between devices: 18.7 us -> 42.8 us  [the longest x1 23.4 us: on_device(): lax.ppermute(other, 'col', [(c, (c - 1) % cols) for c in range(cols)])]
    pallas_call x0 -> x2, Pallas kernels: none -> 22 us  [the longest x1 13 us: run_first(): pl.pallas_call(functools.partial(first_kernel, bs, layers), name='first_p...]
    dot_general x2 -> x0, matrix products: 17.9 us -> none  [kept_product(): jnp.einsum('tkxz,ktzy->txy', left_rows, right_cols, preferred_element_typ...]
    reduce_scatter x1 -> x0, waiting for transfers between devices: 9.83 us -> none  [on_device(): lax.psum_scatter(both_stops, 'layer', scatter_dimension=0, tiled=True)]
    select_n x8 -> x0, other arithmetic: 8.59 us -> none  [the longest x4 8.57 us: densify(): jnp.where(present[:, None, None], picked, jnp.zeros((), blocks.dtype))]
    unnamed x2 -> x6, local copies, waits for them, and re-layouts: 0.01 us -> 3.52 us
    reduce_or x4 -> x0, other arithmetic: 1.71 us -> none  [densify(): present = jnp.any(matches, axis=1)]
  transfers between devices with their start and end apart: 7 -> 6, of which waited for: 3 -> 5; matrix products, arithmetic and copies ran while one was open for 28% -> 0% of each run, Pallas kernels for 0% -> 0%
where the time goes in v1:
time: 83.1 us; the launch traced here: 82.8 us
  waiting for transfers between devices  42.8 us (52%)
  Pallas kernels  22 us (26%)
  starting transfers between devices  10.2 us (12%)
  local copies, waits for them, and re-layouts  3.52 us (4%)
  other arithmetic  2.91 us (4%)
  between operations  1.38 us (2%)
    ppermute x1, waiting for transfers between devices, on_device(): lax.ppermute(other, 'col', [(c, (c - 1) % cols) for c in range(cols)])  23.4 us
    ppermute x1, waiting for transfers between devices, on_device(): moved_blocks = lax.ppermute(a_blocks, ('row', 'col'), to_b)  15.9 us
    pallas_call x1, Pallas kernels, run_first(): pl.pallas_call(functools.partial(first_kernel, bs, layers), name='first_p...  13 us
    pallas_call x1, Pallas kernels, run_second(): pl.pallas_call(functools.partial(second_kernel, bs, layers), name='second...  8.97 us
    ppermute x1, starting transfers between devices, on_device(): moved_blocks = lax.ppermute(a_blocks, ('row', 'col'), to_b)  4.47 us
    unnamed x6, local copies, waits for them, and re-layouts  3.52 us
    ppermute x2, waiting for transfers between devices, layer_sum(): total = total + lax.ppermute(shares[step], 'layer', perm)  2.65 us
    ppermute x1, starting transfers between devices, on_device(): lax.ppermute(other, 'col', [(c, (c - 1) % cols) for c in range(cols)])  1.89 us
  transfers between devices with their start and end apart: 6, of which 5 were waited for; matrix products, arithmetic and copies ran while one was open for 0% of the time, Pallas kernels for 0%

profile of v1, /device:TPU:0, one launch (start us, length us, event | category | flops | bytes accessed | tf_op | source)
XLA Modules:
  0.0 82.8 jit_solution(12554846091009346705)
XLA Ops:
  0.7 0.7 select_reduce_fusion.1
  2.1 0.8 select_reduce_fusion
  2.9 0.0 copy-start
  2.9 1.7 %copy-done = bf16[1,1,1,80,128,128]{5,4,3,2,1,0:T(8,128)(2,1)S(1)} copy-done((bf16[1,1,1,80,128,128]{5,4,3,2,1,0:T(8,128)(2,1)S(1)}, bf16[1,1,1,80,128,128]{5,4,3,2,1,0:T(8,128)(2,1)}, u32[]{:S(2)}) %copy-start) | copy-done | bytes 2621464
  4.6 0.0 copy-start.1
  4.6 1.1 %copy-done.1 = bf16[1,1,1,24,128,128]{5,4,3,2,1,0:T(8,128)(2,1)S(1)} copy-done((bf16[1,1,1,24,128,128]{5,4,3,2,1,0:T(8,128)(2,1)S(1)}, bf16[1,1,1,24,128,128]{5,4,3,2,1,0:T(8,128)(2,1)}, u32[]{:S(2)}) %copy-start.1) | copy-done | bytes 786456
  5.8 0.0 copy-start.2
  5.8 0.7 copy-done.2
  6.4 13.0 %first_product.1 = (f32[16,128,128]{2,1,0:T(8,128)S(1)}, f32[16,128,128]{2,1,0:T(8,128)S(1)}, bf16[8,1024,256]{2,1,0:T(8,128)(2,1)S(1)}) custom-call(s32[32]{0:T(128)S(1)} %broadcast_add_fusion.1.a_slot, s32[128]{0:T(128)S(1)} %broadcast_add_fusion.b_slot, s32[32]{0:T(128)S(1)} %bitcast.15, s32[1]{0:T(128)} %bitcast.6.rot, ...), custom_call_target="tpu_custom_call" | custom-call | flops 2147483648 | bytes 12582912 | tf_op jit(solution)/shard_map/first_product/pallas_call | solution.py:142
  19.4 0.6 collective-permute-start.1
  20.1 4.5 %collective-permute-start = (bf16[24,128,128]{2,1,0:T(8,128)(2,1)S(1)}, bf16[24,128,128]{2,1,0:T(8,128)(2,1)S(1)}, u32[]{:S(2)}, u32[]{:S(2)}) collective-permute-start(bf16[24,128,128]{2,1,0:T(8,128)(2,1)S(1)} %bitcast.14), channel_id=1, source_target_pairs={{8,2},{10,4},{12,6},{14,0},{16,10},{18,12},{20,14},{22,8},{24,18},... | collective-permute-start | bytes 2359304 | tf_op jit(solution)/shard_map/ppermute | solution.py:206
  24.5 1.6 %collective-permute-start.2 = (s32[32]{0:T(128)S(1)}, s32[32]{0:T(128)S(1)}, u32[]{:S(2)}, u32[]{:S(2)}) collective-permute-start(s32[32]{0:T(128)S(1)} %broadcast_add_fusion.1.a_slot), channel_id=1, source_target_pairs={{8,2},{10,4},{12,6},{14,0},{16,10},{18,12},{20,14},{22,8},{24,18},... | collective-permute-start | bytes 392 | tf_op jit(solution)/shard_map/ppermute | solution.py:208
  26.1 1.6 %collective-permute-start.3 = (s32[32]{0:T(128)S(1)}, s32[32]{0:T(128)S(1)}, u32[]{:S(2)}, u32[]{:S(2)}) collective-permute-start(s32[32]{0:T(128)S(1)} %bitcast.16), channel_id=1, source_target_pairs={{0,2},{2,4},{4,6},{6,0},{1,3},{3,5},{5,7},{7,1},{8,10},{10,12},{12... | collective-permute-start | bytes 392 | tf_op jit(solution)/shard_map/ppermute | solution.py:209
  27.7 0.0 collective-permute-done.1
  27.7 0.1 add.33
  27.8 15.9 %collective-permute-done.a_blocks = bf16[24,128,128]{2,1,0:T(8,128)(2,1)S(1)} collective-permute-done((bf16[24,128,128]{2,1,0:T(8,128)(2,1)S(1)}, bf16[24,128,128]{2,1,0:T(8,128)(2,1)S(1)}, u32[]{:S(2)}, u32[]{:S(2)}) %collective-permute-start) | collective-permute-done | bytes 786464 | tf_op jit(solution)/shard_map/ppermute | solution.py:206
  43.7 0.1 collective-permute-done.2.a_slot
  43.8 0.8 collective-permute-done.3.kept
  44.6 9.0 %second_product.1 = (f32[16,128,128]{2,1,0:T(8,128)S(1)}, f32[16,128,128]{2,1,0:T(8,128)S(1)}) custom-call(s32[32]{0:T(128)S(1)} %collective-permute-done.2.a_slot, s32[32]{0:T(128)S(1)} %collective-permute-done.3.kept, s32[1]{0:T(128)} %bitcast.6.rot, bf16[24,128,128]{2,1,0:T(8,128)(2,1)S(1)} %collective-permute-done.a_blocks, ...), custom_call_target="tpu_custom_call" | custom-call | flops 2147483648 | bytes 8388608 | tf_op jit(solution)/shard_map/second_product/pallas_call | solution.py:167
  53.6 0.1 collective-permute-start.4
  53.7 2.6 %collective-permute-done.4 = f32[16,128,128]{2,1,0:T(8,128)S(1)} collective-permute-done((f32[16,128,128]{2,1,0:T(8,128)S(1)}, f32[16,128,128]{2,1,0:T(8,128)S(1)}, u32[]{:S(2)}, u32[]{:S(2)}) %collective-permute-start.4) | collective-permute-done | bytes 1048608 | tf_op jit(solution)/shard_map/ppermute | solution.py:192
  56.3 0.2 add.34
  56.5 1.9 %collective-permute-start.5 = (f32[16,128,128]{2,1,0:T(8,128)S(1)}, f32[16,128,128]{2,1,0:T(8,128)S(1)}, u32[]{:S(2)}, u32[]{:S(2)}) collective-permute-start(f32[16,128,128]{2,1,0:T(8,128)S(1)} %add.34), channel_id=1, source_target_pairs={{0,6},{2,0},{4,2},{6,4},{1,7},{3,1},{5,3},{7,5},{8,14},{10,8},{12,... | collective-permute-start | bytes 3145736 | tf_op jit(solution)/shard_map/ppermute | solution.py:218
  58.4 23.4 %collective-permute-done.5 = f32[16,128,128]{2,1,0:T(8,128)S(1)} collective-permute-done((f32[16,128,128]{2,1,0:T(8,128)S(1)}, f32[16,128,128]{2,1,0:T(8,128)S(1)}, u32[]{:S(2)}, u32[]{:S(2)}) %collective-permute-start.5) | collective-permute-done | bytes 1048608 | tf_op jit(solution)/shard_map/ppermute | solution.py:218
  81.7 1.1 %add_bitcast_fusion = f32[1,1,16,128,128]{4,3,2,1,0:T(8,128)} fusion(f32[16,128,128]{2,1,0:T(8,128)S(1)} %add.33, f32[16,128,128]{2,1,0:T(8,128)S(1)} %collective-permute-done.5), kind=kLoop, calls=%fused_computation | loop fusion | flops 262144 | bytes 3145728 | tf_op jit(solution)/shard_map/broadcast_in_dim | solution.py:219
  (6 shorter events, 0.0 us)
Async XLA Ops:
  2.9 1.7 %copy-start = (bf16[1,1,1,80,128,128]{5,4,3,2,1,0:T(8,128)(2,1)S(1)}, bf16[1,1,1,80,128,128]{5,4,3,2,1,0:T(8,128)(2,1)}, u32[]{:S(2)}) copy-start(bf16[1,1,1,80,128,128]{5,4,3,2,1,0:T(8,128)(2,1)} %param.10) | copy-start | bytes 7864324
  4.6 1.1 %copy-start.1 = (bf16[1,1,1,24,128,128]{5,4,3,2,1,0:T(8,128)(2,1)S(1)}, bf16[1,1,1,24,128,128]{5,4,3,2,1,0:T(8,128)(2,1)}, u32[]{:S(2)}) copy-start(bf16[1,1,1,24,128,128]{5,4,3,2,1,0:T(8,128)(2,1)} %param.7) | copy-start | bytes 2359300
  5.8 0.7 copy-start.2
  19.4 8.2 %collective-permute-start.1 = (f32[16,128,128]{2,1,0:T(8,128)S(1)}, f32[16,128,128]{2,1,0:T(8,128)S(1)}, u32[]{:S(2)}, u32[]{:S(2)}) collective-permute-start(f32[16,128,128]{2,1,0:T(8,128)S(1)} %get-tuple-element.13), channel_id=1, source_target_pairs={{0,1},{1,0},{2,3},{3,2},{4,5},{5,4},{6,7},{7,6},{8,9},{9,8},{10,11... | collective-permute-start | bytes 3145736 | tf_op jit(solution)/shard_map/ppermute | solution.py:192
  20.1 23.7 %collective-permute-start = (bf16[24,128,128]{2,1,0:T(8,128)(2,1)S(1)}, bf16[24,128,128]{2,1,0:T(8,128)(2,1)S(1)}, u32[]{:S(2)}, u32[]{:S(2)}) collective-permute-start(bf16[24,128,128]{2,1,0:T(8,128)(2,1)S(1)} %bitcast.14), channel_id=1, source_target_pairs={{8,2},{10,4},{12,6},{14,0},{16,10},{18,12},{20,14},{22,8},{24,18},... | collective-permute-start | bytes 2359304 | tf_op jit(solution)/shard_map/ppermute | solution.py:206
  24.5 19.3 %collective-permute-start.2 = (s32[32]{0:T(128)S(1)}, s32[32]{0:T(128)S(1)}, u32[]{:S(2)}, u32[]{:S(2)}) collective-permute-start(s32[32]{0:T(128)S(1)} %broadcast_add_fusion.1.a_slot), channel_id=1, source_target_pairs={{8,2},{10,4},{12,6},{14,0},{16,10},{18,12},{20,14},{22,8},{24,18},... | collective-permute-start | bytes 392 | tf_op jit(solution)/shard_map/ppermute | solution.py:208
  26.1 18.5 %collective-permute-start.3 = (s32[32]{0:T(128)S(1)}, s32[32]{0:T(128)S(1)}, u32[]{:S(2)}, u32[]{:S(2)}) collective-permute-start(s32[32]{0:T(128)S(1)} %bitcast.16), channel_id=1, source_target_pairs={{0,2},{2,4},{4,6},{6,0},{1,3},{3,5},{5,7},{7,1},{8,10},{10,12},{12... | collective-permute-start | bytes 392 | tf_op jit(solution)/shard_map/ppermute | solution.py:209
  53.6 2.7 %collective-permute-start.4 = (f32[16,128,128]{2,1,0:T(8,128)S(1)}, f32[16,128,128]{2,1,0:T(8,128)S(1)}, u32[]{:S(2)}, u32[]{:S(2)}) collective-permute-start(f32[16,128,128]{2,1,0:T(8,128)S(1)} %get-tuple-element.18), channel_id=1, source_target_pairs={{0,1},{1,0},{2,3},{3,2},{4,5},{5,4},{6,7},{7,6},{8,9},{9,8},{10,11... | collective-permute-start | bytes 3145736 | tf_op jit(solution)/shard_map/ppermute | solution.py:192
  56.5 25.3 %collective-permute-start.5 = (f32[16,128,128]{2,1,0:T(8,128)S(1)}, f32[16,128,128]{2,1,0:T(8,128)S(1)}, u32[]{:S(2)}, u32[]{:S(2)}) collective-permute-start(f32[16,128,128]{2,1,0:T(8,128)S(1)} %add.34), channel_id=1, source_target_pairs={{0,6},{2,0},{4,2},{6,4},{1,7},{3,1},{5,3},{7,5},{8,14},{10,8},{12,... | collective-permute-start | bytes 3145736 | tf_op jit(solution)/shard_map/ppermute | solution.py:218

commit v2 on v1

--- a/solution.py
+++ b/solution.py
@@ -7,14 +7,17 @@
 from jax.experimental.pallas import tpu as pltpu
 from jax.sharding import PartitionSpec as P
 
+
 CR = 4
 CC = 16
 KW = 8
 PAIR = 2
 GROUPS = CC // PAIR
-
-ANY = pl.BlockSpec(memory_space=pl.ANY)
+SCALE = 16.0
+
+HBM = pl.BlockSpec(memory_space=pltpu.HBM)
 SMEM = pl.BlockSpec(memory_space=pltpu.SMEM)
+VMEM = pl.BlockSpec(memory_space=pltpu.VMEM)
 
 
 def slot_of_cell(cell_list, live_count, cells):
@@ -47,23 +50,6 @@
 def right_cell(right, inner, col, bs):
     start = pl.multiple_of((col % PAIR) * bs, bs)
     return right.at[col // PAIR, pl.ds(inner * bs, bs), pl.ds(start, bs)]
-
-
-def kept_blocks(kept, rot, acc, outs, out_sem):
-    total = sum(out.shape[0] for out in outs)
-    copies = []
-    for place in range(total):
-        cell = kept[lax.rem(place + rot[0], total)]
-        out = outs[place // outs[0].shape[0]]
-        copies.append(
-            pltpu.make_async_copy(
-                acc.at[cell % CC, cell // CC], out.at[place % out.shape[0]], out_sem.at[place]
-            )
-        )
-    for copy in copies:
-        copy.start()
-    for copy in copies:
-        copy.wait()
 
 
 def multiply(left, right, acc, group, bs):
@@ -75,9 +61,17 @@
             ]
 
 
+def put_kept(kept, rot, acc, outs):
+    total = sum(out.shape[0] for out in outs)
+    for place in range(total):
+        cell = kept[lax.rem(place + rot[0], total)]
+        out = outs[place // outs[0].shape[0]]
+        out[place % out.shape[0]] = acc[cell % CC, cell // CC]
+
+
 def first_kernel(bs, layers, a_slot, b_slot, kept, rot, a_blocks, b_blocks, *refs):
     outs, dense = refs[:layers], refs[layers]
-    left, right, acc, a_sem, b_sem, out_sem, dense_sem = refs[layers + 1 :]
+    left, acc, a_sem, b_sem = refs[layers + 1 :]
 
     for cell in range(CR * KW):
         fill_cell(a_slot[cell], a_blocks, left_cell(left, cell, bs), a_sem.at[cell])
@@ -88,7 +82,7 @@
             fill_cell(
                 b_slot[inner * CC + col],
                 b_blocks,
-                right_cell(right, inner, col, bs),
+                right_cell(dense, inner, col, bs),
                 b_sem.at[inner * CC + col],
             )
 
@@ -103,36 +97,28 @@
                 wait_cell(
                     b_slot[inner * CC + col],
                     b_blocks,
-                    right_cell(right, inner, col, bs),
+                    right_cell(dense, inner, col, bs),
                     b_sem.at[inner * CC + col],
                 )
-        multiply(left, right, acc, group, bs)
-
-    dense_copy = pltpu.make_async_copy(right, dense, dense_sem)
-    dense_copy.start()
-    kept_blocks(kept, rot, acc, outs, out_sem)
-    dense_copy.wait()
+        multiply(left, dense, acc, group, bs)
+
+    put_kept(kept, rot, acc, outs)
 
 
 def second_kernel(bs, layers, a_slot, kept, rot, a_blocks, dense, *refs):
     outs = refs[:layers]
-    left, right, acc, a_sem, dense_sem, out_sem = refs[layers:]
+    left, acc = refs[layers:]
 
     for cell in range(CR * KW):
-        fill_cell(a_slot[cell], a_blocks, left_cell(left, cell, bs), a_sem.at[cell])
-
-    for group in range(GROUPS):
-        pltpu.make_async_copy(dense.at[group], right.at[group], dense_sem.at[group]).start()
-
-    for cell in range(CR * KW):
-        wait_cell(a_slot[cell], a_blocks, left_cell(left, cell, bs), a_sem.at[cell])
+        slot = a_slot[cell]
+        block = a_blocks[jnp.maximum(slot, 0)]
+        left_cell(left, cell, bs)[...] = jnp.where(slot >= 0, block, jnp.zeros_like(block))
 
     @pl.loop(0, GROUPS)
     def _(group):
-        pltpu.make_async_copy(dense.at[group], right.at[group], dense_sem.at[group]).wait()
-        multiply(left, right, acc, group, bs)
-
-    kept_blocks(kept, rot, acc, outs, out_sem)
+        multiply(left, dense, acc, group, bs)
+
+    put_kept(kept, rot, acc, outs)
 
 
 def run_first(layers, a_slot, b_slot, kept, rot, a_blocks, b_blocks):
@@ -143,16 +129,13 @@
         functools.partial(first_kernel, bs, layers),
         name="first_product",
         out_shape=[share] * layers + [dense],
-        in_specs=[SMEM] * 4 + [ANY] * 2,
-        out_specs=[ANY] * (layers + 1),
+        in_specs=[SMEM] * 4 + [HBM] * 2,
+        out_specs=[VMEM] * (layers + 1),
         scratch_shapes=[
             pltpu.VMEM((CR * bs, KW * bs), a_blocks.dtype),
-            pltpu.VMEM(dense.shape, dense.dtype),
             pltpu.VMEM((CC, CR, bs, bs), jnp.float32),
             pltpu.SemaphoreType.DMA((CR * KW,)),
             pltpu.SemaphoreType.DMA((KW * CC,)),
-            pltpu.SemaphoreType.DMA((capacity,)),
-            pltpu.SemaphoreType.DMA,
         ],
         compiler_params=pltpu.CompilerParams(vmem_limit_bytes=24 << 20),
         cost_estimate=pl.CostEstimate(
@@ -168,15 +151,11 @@
         functools.partial(second_kernel, bs, layers),
         name="second_product",
         out_shape=[share] * layers,
-        in_specs=[SMEM] * 3 + [ANY] * 2,
-        out_specs=[ANY] * layers,
+        in_specs=[SMEM] * 3 + [VMEM] * 2,
+        out_specs=[VMEM] * layers,
         scratch_shapes=[
             pltpu.VMEM((CR * bs, KW * bs), a_blocks.dtype),
-            pltpu.VMEM(dense.shape, dense.dtype),
             pltpu.VMEM((CC, CR, bs, bs), jnp.float32),
-            pltpu.SemaphoreType.DMA((CR * KW,)),
-            pltpu.SemaphoreType.DMA((GROUPS,)),
-            pltpu.SemaphoreType.DMA((capacity,)),
         ],
         compiler_params=pltpu.CompilerParams(vmem_limit_bytes=24 << 20),
         cost_estimate=pl.CostEstimate(
@@ -203,20 +182,23 @@
         for r in range(rows)
         for c in range(cols)
     ]
-    moved_blocks = lax.ppermute(a_blocks, ("row", "col"), to_b)
     a_slot = slot_of_cell(a_cells, a_count, CR * KW)
-    moved_slot = lax.ppermute(a_slot, ("row", "col"), to_b)
-    moved_kept = lax.ppermute(kept, "col", [(c, (c + 1) % cols) for c in range(cols)])
-
     b_slot = slot_of_cell(b_cells, b_count, KW * CC)
     rot = (lax.axis_index("layer") * (kept.shape[0] // layers)).astype(jnp.int32).reshape(1)
+    to_next = [(c, (c + 1) % cols) for c in range(cols)]
+    to_last = [(c, (c - 1) % cols) for c in range(cols)]
+    moved_blocks = lax.ppermute(a_blocks, ("row", "col"), to_b)
+    moved_slot = lax.ppermute(a_slot, ("row", "col"), to_b)
+    moved_kept = lax.ppermute(kept, "col", to_next)
     *first, dense = run_first(layers, a_slot, b_slot, kept, rot, a_blocks, b_blocks)
     own = layer_sum(first, layers)
     moved_blocks, own = lax.optimization_barrier((moved_blocks, own))
     second = run_second(layers, moved_slot, moved_kept, rot, moved_blocks, dense)
     other = layer_sum(second, layers)
-    back = lax.ppermute(other, "col", [(c, (c - 1) % cols) for c in range(cols)])
-    return (own + back)[None, None]
+    sent = (other * SCALE).astype(jnp.float16)
+    back = lax.ppermute(sent, "col", to_last)
+    total = own + back.astype(jnp.float32) * (1.0 / SCALE)
+    return total[None, None]
 
 
 def solution(mesh):

time: 83.1 us -> 64 us (0.77)
  waiting for transfers between devices: 42.8 us -> 31.6 us
  Pallas kernels: 22 us -> 14.1 us
    ppermute x2, waiting for transfers between devices: 24.2 us -> 12.9 us  [the longest x1 12.2 us: on_device(): back = lax.ppermute(sent, 'col', to_last)]
    pallas_call x1, Pallas kernels: 8.97 us -> 4.71 us  [run_second(): pl.pallas_call(functools.partial(second_kernel, bs, layers), name='second...]
    pallas_call x1, Pallas kernels: 13 us -> 9.36 us  [run_first(): pl.pallas_call(functools.partial(first_kernel, bs, layers), name='first_p...]
where the time goes in v2:
time: 64 us; the launch traced here: 63.7 us
  waiting for transfers between devices  31.6 us (49%)
  Pallas kernels  14.1 us (22%)
  starting transfers between devices  10.2 us (16%)
  local copies, waits for them, and re-layouts  3.52 us (6%)
  other arithmetic  2.97 us (5%)
  between operations  1.38 us (2%)
    ppermute x1, waiting for transfers between devices, on_device(): moved_blocks = lax.ppermute(a_blocks, ('row', 'col'), to_b)  16 us
    ppermute x1, waiting for transfers between devices, on_device(): back = lax.ppermute(sent, 'col', to_last)  12.2 us
    pallas_call x1, Pallas kernels, run_first(): pl.pallas_call(functools.partial(first_kernel, bs, layers), name='first_p...  9.36 us
    pallas_call x1, Pallas kernels, run_second(): pl.pallas_call(functools.partial(second_kernel, bs, layers), name='second...  4.71 us
    ppermute x1, starting transfers between devices, on_device(): moved_blocks = lax.ppermute(a_blocks, ('row', 'col'), to_b)  4.52 us
    unnamed x6, local copies, waits for them, and re-layouts  3.52 us
    ppermute x2, waiting for transfers between devices, layer_sum(): total = total + lax.ppermute(shares[step], 'layer', perm)  2.65 us
    ppermute x1, starting transfers between devices, on_device(): back = lax.ppermute(sent, 'col', to_last)  1.86 us
  transfers between devices with their start and end apart: 6, of which 5 were waited for; matrix products, arithmetic and copies ran while one was open for 0% of the time, Pallas kernels for 0%

profile of v2, /device:TPU:0, one launch (start us, length us, event | category | flops | bytes accessed | tf_op | source)
XLA Modules:
  0.0 63.7 jit_solution(12032102915195059917)
XLA Ops:
  0.7 0.7 %select_reduce_fusion.1 = s32[32]{0:T(128)S(1)} fusion(s32[24]{0:T(128)S(1)} %iota_add_fusion.1, s32[24]{0:T(128)} %bitcast.17, pred[24]{0:T(512)(128)(4,1)S(1)} %iota_compare_fusion.3), kind=kLoop, calls=%fused_computation.5 | loop fusion | flops 3040 | bytes 344 | tf_op jit(solution)/shard_map/reduce_sum | solution.py:27
  2.1 0.8 %select_reduce_fusion = s32[128]{0:T(128)S(1)} fusion(s32[80]{0:T(128)S(1)} %iota_add_fusion, s32[80]{0:T(128)} %bitcast.18, pred[80]{0:T(512)(128)(4,1)S(1)} %iota_compare_fusion.2), kind=kLoop, calls=%fused_computation.2 | loop fusion | flops 40832 | bytes 1232 | tf_op jit(solution)/shard_map/reduce_sum | solution.py:27
  2.9 0.0 copy-start
  2.9 1.7 %copy-done = bf16[1,1,1,80,128,128]{5,4,3,2,1,0:T(8,128)(2,1)S(1)} copy-done((bf16[1,1,1,80,128,128]{5,4,3,2,1,0:T(8,128)(2,1)S(1)}, bf16[1,1,1,80,128,128]{5,4,3,2,1,0:T(8,128)(2,1)}, u32[]{:S(2)}) %copy-start) | copy-done | bytes 2621464
  4.6 0.0 copy-start.1
  4.6 1.1 %copy-done.1 = bf16[1,1,1,24,128,128]{5,4,3,2,1,0:T(8,128)(2,1)S(1)} copy-done((bf16[1,1,1,24,128,128]{5,4,3,2,1,0:T(8,128)(2,1)S(1)}, bf16[1,1,1,24,128,128]{5,4,3,2,1,0:T(8,128)(2,1)}, u32[]{:S(2)}) %copy-start.1) | copy-done | bytes 786456
  5.8 0.0 copy-start.2
  5.8 0.7 %copy-done.2 = s32[1,1,32]{2,1,0:T(1,128)S(1)} copy-done((s32[1,1,32]{2,1,0:T(1,128)S(1)}, s32[1,1,32]{2,1,0:T(1,128)}, u32[]{:S(2)}) %copy-start.2) | copy-done | bytes 152
  6.4 9.4 %first_product.1 = (f32[16,128,128]{2,1,0:T(8,128)S(1)}, f32[16,128,128]{2,1,0:T(8,128)S(1)}, bf16[8,1024,256]{2,1,0:T(8,128)(2,1)S(1)}) custom-call(s32[32]{0:T(128)S(1)} %broadcast_add_fusion.1.a_slot, s32[128]{0:T(128)S(1)} %broadcast_add_fusion.b_slot, s32[32]{0:T(128)S(1)} %bitcast.15, s32[1]{0:T(128)} %bitcast.6.rot, ...), custom_call_target="tpu_custom_call" | custom-call | flops 2147483648 | bytes 12582912 | tf_op jit(solution)/shard_map/first_product/pallas_call | solution.py:128
  15.8 0.6 collective-permute-start.1
  16.4 4.5 %collective-permute-start = (bf16[24,128,128]{2,1,0:T(8,128)(2,1)S(1)}, bf16[24,128,128]{2,1,0:T(8,128)(2,1)S(1)}, u32[]{:S(2)}, u32[]{:S(2)}) collective-permute-start(bf16[24,128,128]{2,1,0:T(8,128)(2,1)S(1)} %bitcast.14), channel_id=1, source_target_pairs={{8,2},{10,4},{12,6},{14,0},{16,10},{18,12},{20,14},{22,8},{24,18},... | collective-permute-start | bytes 2359304 | tf_op jit(solution)/shard_map/ppermute | solution.py:190
  20.9 1.5 %collective-permute-start.2 = (s32[32]{0:T(128)S(1)}, s32[32]{0:T(128)S(1)}, u32[]{:S(2)}, u32[]{:S(2)}) collective-permute-start(s32[32]{0:T(128)S(1)} %broadcast_add_fusion.1.a_slot), channel_id=1, source_target_pairs={{8,2},{10,4},{12,6},{14,0},{16,10},{18,12},{20,14},{22,8},{24,18},... | collective-permute-start | bytes 392 | tf_op jit(solution)/shard_map/ppermute | solution.py:191
  22.4 1.6 %collective-permute-start.3 = (s32[32]{0:T(128)S(1)}, s32[32]{0:T(128)S(1)}, u32[]{:S(2)}, u32[]{:S(2)}) collective-permute-start(s32[32]{0:T(128)S(1)} %bitcast.16), channel_id=1, source_target_pairs={{0,2},{2,4},{4,6},{6,0},{1,3},{3,5},{5,7},{7,1},{8,10},{10,12},{12... | collective-permute-start | bytes 392 | tf_op jit(solution)/shard_map/ppermute | solution.py:192
  24.0 0.0 collective-permute-done.1
  24.0 0.1 add.33
  24.1 16.0 %collective-permute-done.a_blocks = bf16[24,128,128]{2,1,0:T(8,128)(2,1)S(1)} collective-permute-done((bf16[24,128,128]{2,1,0:T(8,128)(2,1)S(1)}, bf16[24,128,128]{2,1,0:T(8,128)(2,1)S(1)}, u32[]{:S(2)}, u32[]{:S(2)}) %collective-permute-start) | collective-permute-done | bytes 786464 | tf_op jit(solution)/shard_map/ppermute | solution.py:190
  40.1 0.1 collective-permute-done.2.a_slot
  40.2 0.8 %collective-permute-done.3.kept = s32[32]{0:T(128)S(1)} collective-permute-done((s32[32]{0:T(128)S(1)}, s32[32]{0:T(128)S(1)}, u32[]{:S(2)}, u32[]{:S(2)}) %collective-permute-start.3) | collective-permute-done | bytes 160 | tf_op jit(solution)/shard_map/ppermute | solution.py:192
  41.0 4.7 %second_product.1 = (f32[16,128,128]{2,1,0:T(8,128)S(1)}, f32[16,128,128]{2,1,0:T(8,128)S(1)}) custom-call(s32[32]{0:T(128)S(1)} %collective-permute-done.2.a_slot, s32[32]{0:T(128)S(1)} %collective-permute-done.3.kept, s32[1]{0:T(128)} %bitcast.6.rot, bf16[24,128,128]{2,1,0:T(8,128)(2,1)S(1)} %collective-permute-done.a_blocks, ...), custom_call_target="tpu_custom_call" | custom-call | flops 2147483648 | bytes 8388608 | tf_op jit(solution)/shard_map/second_product/pallas_call | solution.py:150
  45.7 0.1 collective-permute-start.4
  45.8 2.6 %collective-permute-done.4 = f32[16,128,128]{2,1,0:T(8,128)S(1)} collective-permute-done((f32[16,128,128]{2,1,0:T(8,128)S(1)}, f32[16,128,128]{2,1,0:T(8,128)S(1)}, u32[]{:S(2)}, u32[]{:S(2)}) %collective-permute-start.4) | collective-permute-done | bytes 1048608 | tf_op jit(solution)/shard_map/ppermute | solution.py:171
  48.4 0.2 multiply_convert_fusion
  48.6 1.9 %collective-permute-start.5 = (f16[16,128,128]{2,1,0:T(8,128)(2,1)S(1)}, f16[16,128,128]{2,1,0:T(8,128)(2,1)S(1)}, u32[]{:S(2)}, u32[]{:S(2)}) collective-permute-start(f16[16,128,128]{2,1,0:T(8,128)(2,1)S(1)} %multiply_convert_fusion), channel_id=1, source_target_pairs={{0,6},{2,0},{4,2},{6,4},{1,7},{3,1},{5,3},{7,5},{8,14},{10,8},{12,... | collective-permute-start | bytes 1572872 | tf_op jit(solution)/shard_map/ppermute | solution.py:199
  50.5 12.2 %collective-permute-done.5 = f16[16,128,128]{2,1,0:T(8,128)(2,1)S(1)} collective-permute-done((f16[16,128,128]{2,1,0:T(8,128)(2,1)S(1)}, f16[16,128,128]{2,1,0:T(8,128)(2,1)S(1)}, u32[]{:S(2)}, u32[]{:S(2)}) %collective-permute-start.5) | collective-permute-done | bytes 524320 | tf_op jit(solution)/shard_map/ppermute | solution.py:199
  62.6 1.1 %add_bitcast_fusion = f32[1,1,16,128,128]{4,3,2,1,0:T(8,128)} fusion(f32[16,128,128]{2,1,0:T(8,128)S(1)} %add.33, f16[16,128,128]{2,1,0:T(8,128)(2,1)S(1)} %collective-permute-done.5), kind=kLoop, calls=%fused_computation | loop fusion | flops 786432 | bytes 2621440 | tf_op jit(solution)/shard_map/broadcast_in_dim | solution.py:201
  (6 shorter events, 0.0 us)
Async XLA Ops:
  2.9 1.7 %copy-start = (bf16[1,1,1,80,128,128]{5,4,3,2,1,0:T(8,128)(2,1)S(1)}, bf16[1,1,1,80,128,128]{5,4,3,2,1,0:T(8,128)(2,1)}, u32[]{:S(2)}) copy-start(bf16[1,1,1,80,128,128]{5,4,3,2,1,0:T(8,128)(2,1)} %param.10) | copy-start | bytes 7864324
  4.6 1.1 %copy-start.1 = (bf16[1,1,1,24,128,128]{5,4,3,2,1,0:T(8,128)(2,1)S(1)}, bf16[1,1,1,24,128,128]{5,4,3,2,1,0:T(8,128)(2,1)}, u32[]{:S(2)}) copy-start(bf16[1,1,1,24,128,128]{5,4,3,2,1,0:T(8,128)(2,1)} %param.7) | copy-start | bytes 2359300
  5.8 0.7 %copy-start.2 = (s32[1,1,32]{2,1,0:T(1,128)S(1)}, s32[1,1,32]{2,1,0:T(1,128)}, u32[]{:S(2)}) copy-start(s32[1,1,32]{2,1,0:T(1,128)} %param.13) | copy-start | bytes 388
  15.8 8.2 %collective-permute-start.1 = (f32[16,128,128]{2,1,0:T(8,128)S(1)}, f32[16,128,128]{2,1,0:T(8,128)S(1)}, u32[]{:S(2)}, u32[]{:S(2)}) collective-permute-start(f32[16,128,128]{2,1,0:T(8,128)S(1)} %get-tuple-element.13), channel_id=1, source_target_pairs={{0,1},{1,0},{2,3},{3,2},{4,5},{5,4},{6,7},{7,6},{8,9},{9,8},{10,11... | collective-permute-start | bytes 3145736 | tf_op jit(solution)/shard_map/ppermute | solution.py:171
  16.4 23.7 %collective-permute-start = (bf16[24,128,128]{2,1,0:T(8,128)(2,1)S(1)}, bf16[24,128,128]{2,1,0:T(8,128)(2,1)S(1)}, u32[]{:S(2)}, u32[]{:S(2)}) collective-permute-start(bf16[24,128,128]{2,1,0:T(8,128)(2,1)S(1)} %bitcast.14), channel_id=1, source_target_pairs={{8,2},{10,4},{12,6},{14,0},{16,10},{18,12},{20,14},{22,8},{24,18},... | collective-permute-start | bytes 2359304 | tf_op jit(solution)/shard_map/ppermute | solution.py:190
  20.9 19.3 %collective-permute-start.2 = (s32[32]{0:T(128)S(1)}, s32[32]{0:T(128)S(1)}, u32[]{:S(2)}, u32[]{:S(2)}) collective-permute-start(s32[32]{0:T(128)S(1)} %broadcast_add_fusion.1.a_slot), channel_id=1, source_target_pairs={{8,2},{10,4},{12,6},{14,0},{16,10},{18,12},{20,14},{22,8},{24,18},... | collective-permute-start | bytes 392 | tf_op jit(solution)/shard_map/ppermute | solution.py:191
  22.4 18.6 %collective-permute-start.3 = (s32[32]{0:T(128)S(1)}, s32[32]{0:T(128)S(1)}, u32[]{:S(2)}, u32[]{:S(2)}) collective-permute-start(s32[32]{0:T(128)S(1)} %bitcast.16), channel_id=1, source_target_pairs={{0,2},{2,4},{4,6},{6,0},{1,3},{3,5},{5,7},{7,1},{8,10},{10,12},{12... | collective-permute-start | bytes 392 | tf_op jit(solution)/shard_map/ppermute | solution.py:192
  45.7 2.7 %collective-permute-start.4 = (f32[16,128,128]{2,1,0:T(8,128)S(1)}, f32[16,128,128]{2,1,0:T(8,128)S(1)}, u32[]{:S(2)}, u32[]{:S(2)}) collective-permute-start(f32[16,128,128]{2,1,0:T(8,128)S(1)} %get-tuple-element.18), channel_id=1, source_target_pairs={{0,1},{1,0},{2,3},{3,2},{4,5},{5,4},{6,7},{7,6},{8,9},{9,8},{10,11... | collective-permute-start | bytes 3145736 | tf_op jit(solution)/shard_map/ppermute | solution.py:171
  48.6 14.0 %collective-permute-start.5 = (f16[16,128,128]{2,1,0:T(8,128)(2,1)S(1)}, f16[16,128,128]{2,1,0:T(8,128)(2,1)S(1)}, u32[]{:S(2)}, u32[]{:S(2)}) collective-permute-start(f16[16,128,128]{2,1,0:T(8,128)(2,1)S(1)} %multiply_convert_fusion), channel_id=1, source_target_pairs={{0,6},{2,0},{4,2},{6,4},{1,7},{3,1},{5,3},{7,5},{8,14},{10,8},{12,... | collective-permute-start | bytes 1572872 | tf_op jit(solution)/shard_map/ppermute | solution.py:199

commit v3 on v2

v3 whole, which is shorter than its diff:
```python
import functools

import jax
import jax.numpy as jnp
from jax import lax
from jax.experimental import pallas as pl
from jax.experimental.pallas import tpu as pltpu
from jax.sharding import PartitionSpec as P


CR = 4
CC = 16
KW = 8
PAIR = 2
GROUPS = CC // PAIR
F16_TOP = 32768.0

HBM = pl.BlockSpec(memory_space=pltpu.HBM)
SMEM = pl.BlockSpec(memory_space=pltpu.SMEM)
VMEM = pl.BlockSpec(memory_space=pltpu.VMEM)


def fill_table(table, cell_list, count):
    for cell in range(table.shape[0]):
        table[cell] = -1

    @pl.loop(0, count[0])
    def _(slot):
        table[cell_list[slot]] = slot


def fill_cell(slot, blocks, target, sem):
    @pl.when(slot >= 0)
    def _():
        pltpu.make_async_copy(blocks.at[slot], target, sem).start()

    @pl.when(slot < 0)
    def _():
        target[...] = jnp.zeros(target.shape, target.dtype)


def wait_cell(slot, blocks, target, sem):
    @pl.when(slot >= 0)
    def _():
        pltpu.make_async_copy(blocks.at[slot], target, sem).wait()


def left_cell(left, cell, bs):
    return left.at[pl.ds((cell // KW) * bs, bs), pl.ds((cell % KW) * bs, bs)]


def right_cell(right, inner, col, bs):
    start = pl.multiple_of((col % PAIR) * bs, bs)
    return right.at[col // PAIR, pl.ds(inner * bs, bs), pl.ds(start, bs)]


def multiply(left, right, acc, group, bs):
    product = jnp.dot(left[...], right[group], preferred_element_type=jnp.float32)
    for half in range(PAIR):
        for row in range(CR):
            acc[group * PAIR + half, row] = product[
                row * bs : (row + 1) * bs, half * bs : (half + 1) * bs
            ]


def put_kept(cells, rot, acc, outs, first):
    total = cells.shape[0]
    share = total // len(outs)
    for step, out in enumerate(outs):
        for place in range(out.shape[0]):
            cell = cells[lax.rem(step * share + first + place + rot[0], total)]
            out[place] = acc[cell % CC, cell // CC]


def groups_for(cells, layers, head):
    share = cells.shape[0] // layers
    last = [(cells[layer * share + head - 1] % CC) // PAIR for layer in range(layers)]
    return functools.reduce(jnp.maximum, last) + 1


def peak(value):
    return jnp.max(jnp.abs(value.astype(jnp.float32)))


def first_kernel(bs, layers, a_cells, a_count, b_cells, b_count, cells, rot, a_blocks, b_blocks, *refs):
    outs, (dense, peaks) = refs[:layers], refs[layers : layers + 2]
    left, acc, a_slot, b_slot, a_sem, b_sem = refs[layers + 2 :]

    fill_table(a_slot, a_cells, a_count)
    fill_table(b_slot, b_cells, b_count)
    for cell in range(CR * KW):
        fill_cell(a_slot[cell], a_blocks, left_cell(left, cell, bs), a_sem.at[cell])

    @pl.loop(0, CC)
    def _(col):
        for inner in range(KW):
            fill_cell(
                b_slot[inner * CC + col],
                b_blocks,
                right_cell(dense, inner, col, bs),
                b_sem.at[inner * CC + col],
            )

    for cell in range(CR * KW):
        wait_cell(a_slot[cell], a_blocks, left_cell(left, cell, bs), a_sem.at[cell])

    def group_step(group, top):
        for half in range(PAIR):
            col = group * PAIR + half
            for inner in range(KW):
                wait_cell(
                    b_slot[inner * CC + col],
                    b_blocks,
                    right_cell(dense, inner, col, bs),
                    b_sem.at[inner * CC + col],
                )
        multiply(left, dense, acc, group, bs)
        return jnp.maximum(top, peak(dense[group]))

    peaks[0] = peak(left[...])
    peaks[1] = lax.fori_loop(0, GROUPS, group_step, jnp.float32(0))
    put_kept(cells, rot, acc, outs, 0)


def head_kernel(bs, layers, a_cells, a_count, cells, rot, a_blocks, dense, *refs):
    outs, (left, acc, a_slot) = refs[:layers], refs[layers:]
    fill_table(a_slot, a_cells, a_count)
    for cell in range(CR * KW):
        slot = a_slot[cell]
        block = a_blocks[jnp.maximum(slot, 0)]
        left_cell(left, cell, bs)[...] = jnp.where(slot >= 0, block, jnp.zeros_like(block))

    @pl.loop(0, groups_for(cells, layers, outs[0].shape[0]))
    def _(group):
        multiply(left, dense, acc, group, bs)

    put_kept(cells, rot, acc, outs, 0)


def tail_kernel(bs, layers, head, cells, rot, left, dense, acc_in, *refs):
    outs, acc = refs[:layers], refs[layers]

    @pl.loop(groups_for(cells, layers, head), GROUPS)
    def _(group):
        multiply(left, dense, acc, group, bs)

    put_kept(cells, rot, acc, outs, head)


def scatter_kernel(places, blocks, *refs):
    out, sem = refs[-2:]
    copies = [
        pltpu.make_async_copy(blocks.at[i], out.at[places[i]], sem.at[i])
        for i in range(blocks.shape[0])
    ]
    for copy in copies:
        copy.start()
    for copy in copies:
        copy.wait()


def cost(share, bytes_accessed, bs):
    flops = int(share * 2 * CR * KW * CC * bs**3)
    return pl.CostEstimate(flops=flops, bytes_accessed=bytes_accessed, transcendentals=0)


def shares(count, layers, bs):
    return [jax.ShapeDtypeStruct((count, bs, bs), jnp.float32)] * layers


def run_first(layers, a_cells, a_count, b_cells, b_count, cells, rot, a_blocks, b_blocks):
    bs = a_blocks.shape[-1]
    dense = jax.ShapeDtypeStruct((GROUPS, KW * bs, PAIR * bs), b_blocks.dtype)
    *outs, dense, peaks = pl.pallas_call(
        functools.partial(first_kernel, bs, layers),
        name="first_product",
        out_shape=shares(cells.shape[0] // layers, layers, bs)
        + [dense, jax.ShapeDtypeStruct((2,), jnp.float32)],
        in_specs=[SMEM] * 6 + [HBM] * 2,
        out_specs=[VMEM] * (layers + 1) + [SMEM],
        scratch_shapes=[
            pltpu.VMEM((CR * bs, KW * bs), a_blocks.dtype),
            pltpu.VMEM((CC, CR, bs, bs), jnp.float32),
            pltpu.SMEM((CR * KW,), jnp.int32),
            pltpu.SMEM((KW * CC,), jnp.int32),
            pltpu.SemaphoreType.DMA((CR * KW,)),
            pltpu.SemaphoreType.DMA((KW * CC,)),
        ],
        compiler_params=pltpu.CompilerParams(vmem_limit_bytes=24 << 20),
        cost_estimate=cost(1, 12 << 20, bs),
    )(a_cells, a_count, b_cells, b_count, cells, rot, a_blocks, b_blocks)
    return outs, dense, peaks


def run_head(layers, head, a_cells, a_count, cells, rot, a_blocks, dense):
    bs = a_blocks.shape[-1]
    left = jax.ShapeDtypeStruct((CR * bs, KW * bs), a_blocks.dtype)
    acc = jax.ShapeDtypeStruct((CC, CR, bs, bs), jnp.float32)
    *outs, left, acc = pl.pallas_call(
        functools.partial(head_kernel, bs, layers),
        name="head_product",
        out_shape=shares(head, layers, bs) + [left, acc],
        in_specs=[SMEM] * 4 + [VMEM] * 2,
        out_specs=[VMEM] * (layers + 2),
        scratch_shapes=[pltpu.SMEM((CR * KW,), jnp.int32)],
        compiler_params=pltpu.CompilerParams(vmem_limit_bytes=24 << 20),
        cost_estimate=cost(0.5, 4 << 20, bs),
    )(a_cells, a_count, cells, rot, a_blocks, dense)
    return outs, left, acc


def run_tail(layers, head, cells, rot, left, dense, acc):
    bs = acc.shape[-1]
    tail = cells.shape[0] // layers - head
    *outs, _ = pl.pallas_call(
        functools.partial(tail_kernel, bs, layers, head),
        name="tail_product",
        out_shape=shares(tail, layers, bs) + [jax.ShapeDtypeStruct(acc.shape, acc.dtype)],
        in_specs=[SMEM] * 2 + [VMEM] * 3,
        out_specs=[VMEM] * (layers + 1),
        input_output_aliases={4: layers},
        compiler_params=pltpu.CompilerParams(vmem_limit_bytes=24 << 20),
        cost_estimate=cost(0.5, 4 << 20, bs),
    )(cells, rot, left, dense, acc)
    return outs


def scatter_blocks(places, blocks, out, capacity):
    shape = jax.ShapeDtypeStruct((capacity,) + blocks.shape[1:], blocks.dtype)
    held = [] if out is None else [out]
    return pl.pallas_call(
        scatter_kernel,
        name="scatter_blocks",
        out_shape=shape,
        in_specs=[SMEM, VMEM] + [HBM] * len(held),
        out_specs=HBM,
        scratch_shapes=[pltpu.SemaphoreType.DMA((blocks.shape[0],))],
        input_output_aliases={2: 0} if held else {},
        compiler_params=pltpu.CompilerParams(vmem_limit_bytes=4 << 20),
    )(places, blocks, *held)


def column_order(kept, layers):
    share = kept.shape[0] // layers
    lists = kept.reshape(layers, share)
    ids = jnp.arange(share, dtype=jnp.int32)
    keys = (lists % CC) * share + ids[None, :]
    rank = jnp.sum((keys[:, None, :] < keys[:, :, None]).astype(jnp.int32), axis=2)
    at_rank = rank[:, None, :] == ids[None, :, None]
    both = jnp.stack([lists, jnp.broadcast_to(ids[None, :], lists.shape)])
    return jnp.sum(jnp.where(at_rank[None], both[:, :, None, :], 0), axis=3).reshape(2, -1)


def over_layers(combine, values, layers):
    total = values[0]
    for step in range(1, layers):
        perm = [(i, (i + step) % layers) for i in range(layers)]
        total = combine(total, lax.ppermute(values[step], "layer", perm))
    return total


def narrow(value, scale):
    return lax.reduce_precision(value * scale, 8, 10).astype(jnp.float16)


def on_device(rows, cols, layers, a_blocks, a_cells, a_count, b_blocks, b_cells, b_count, c_cells):
    a_blocks, a_cells, a_count = a_blocks[0, 0, 0], a_cells[0, 0, 0], a_count[0, 0]
    b_blocks, b_cells, b_count = b_blocks[0, 0, 0], b_cells[0, 0, 0], b_count[0, 0]
    kept = c_cells[0, 0]

    to_b = [
        (((r + 1) % rows) * cols + c, r * cols + (c + 1) % cols)
        for r in range(rows)
        for c in range(cols)
    ]
    to_next = [(c, (c + 1) % cols) for c in range(cols)]
    to_last = [(c, (c - 1) % cols) for c in range(cols)]
    share = kept.shape[0] // layers
    head = (share + 1) // 2
    inner = KW * a_blocks.shape[-1]

    moved_blocks = lax.ppermute(a_blocks, ("row", "col"), to_b)
    moved_slots = lax.ppermute((a_cells, a_count), ("row", "col"), to_b)
    cells, places = column_order(kept, layers)
    layer = lax.axis_index("layer").astype(jnp.int32)
    rot = (layer * share).reshape(1)
    own_places = lax.dynamic_slice(places, (layer * share,), (share,))
    moved_cells = lax.ppermute(cells, "col", to_next)
    first, dense, peaks = run_first(
        layers,
        a_cells,
        a_count,
        b_cells,
        b_count,
        cells,
        rot,
        pltpu.with_memory_space_constraint(a_blocks, pltpu.HBM),
        pltpu.with_memory_space_constraint(b_blocks, pltpu.HBM),
    )
    own = over_layers(jnp.add, first, layers)
    peaks = over_layers(jnp.maximum, [peaks] * layers, layers)
    moved_blocks, own, peaks = lax.optimization_barrier((moved_blocks, own, peaks))
    moved_peak = lax.ppermute(peaks[:1], ("row", "col"), to_b)
    bound = jnp.maximum(layers * inner * moved_peak * peaks[1:], 1e-30)
    heads, left, acc = run_head(layers, head, *moved_slots, moved_cells, rot, moved_blocks, dense)
    other_head = over_layers(jnp.add, heads, layers)
    back_head = lax.ppermute(narrow(other_head, F16_TOP / bound), "col", to_last)
    back_bound = lax.ppermute(bound, "col", to_last)
    tails = run_tail(layers, head, moved_cells, rot, left, dense, acc)
    other_tail = over_layers(jnp.add, tails, layers)
    back_tail = lax.ppermute(narrow(other_tail, F16_TOP / bound), "col", to_last)
    unscale = back_bound * (1.0 / F16_TOP)
    total = own[:head] + back_head.astype(jnp.float32) * unscale
    out = scatter_blocks(own_places[:head], total, None, share)
    back_tail, out = lax.optimization_barrier((back_tail, out))
    total = own[head:] + back_tail.astype(jnp.float32) * unscale
    out = scatter_blocks(own_places[head:], total, out, share)
    return out[None, None]


def solution(mesh):
    sizes = mesh.shape
    return jax.shard_map(
        functools.partial(on_device, sizes["row"], sizes["col"], sizes["layer"]),
        mesh=mesh,
        in_specs=(
            P("row", "col", "layer", None, None, None),
            P("row", "col", "layer", None),
            P("row", "col", "layer"),
            P("row", "col", "layer", None, None, None),
            P("row", "col", "layer", None),
            P("row", "col", "layer"),
            P("row", "col", None),
        ),
        out_specs=P("row", "col", "layer", None, None),
        check_vma=False,
    )
```

time: 64 us -> 73.9 us (1.15)
  starting transfers between devices: 10.2 us -> 21.8 us
  waiting for transfers between devices: 31.6 us -> 21.9 us
  Pallas kernels: 14.1 us -> 18.7 us
  between operations: 1.38 us -> 3.34 us
  other arithmetic: 2.97 us -> 4.41 us
    ppermute x5 -> x11, starting transfers between devices: 5.63 us -> 17.2 us  [the longest x1 9.22 us: on_device(): back_bound = lax.ppermute(bound, 'col', to_last)]
    ppermute x5 -> x11, waiting for transfers between devices: 15.7 us -> 7.97 us  [the longest x1 4.59 us: on_device(): moved_peak = lax.ppermute(peaks[:1], ('row', 'col'), to_b)]
    pallas_call x1 -> x4, Pallas kernels: 4.71 us -> 8.84 us  [the longest x1 3.58 us: run_head(): pl.pallas_call(functools.partial(head_kernel, bs, layers), name='head_pro...]
    convert_element_type x1 -> x2, other arithmetic: 0.18 us -> 2.47 us  [narrow(): return lax.reduce_precision(value * scale, 8, 10).astype(jnp.float16)]
    ppermute x1, waiting for transfers between devices: 16 us -> 13.9 us  [on_device(): moved_blocks = lax.ppermute(a_blocks, ('row', 'col'), to_b)]
    unnamed x6 -> x7, local copies, waits for them, and re-layouts: 3.52 us -> 1.82 us
    unnamed x0 -> x1, other arithmetic: none -> 1.32 us
    reduce_sum x2, other arithmetic: 1.51 us -> 0.33 us  [the longest x1 0.18 us: column_order(): jnp.sum((keys[:, None, :] < keys[:, :, None]).astype(jnp.int32), axis=2)]
  transfers between devices with their start and end apart: 6 -> 12, of which waited for: 5 -> 6; matrix products, arithmetic and copies ran while one was open for 0% -> 5% of each run, Pallas kernels for 0% -> 5%
where the time goes in v3:
time: 73.9 us; the launch traced here: 73.6 us
  waiting for transfers between devices  21.9 us (30%)
  starting transfers between devices  21.8 us (29%)
  Pallas kernels  18.7 us (25%)
  other arithmetic  4.41 us (6%)
  local copies, waits for them, and re-layouts  3.55 us (5%)
  between operations  3.34 us (5%)
    ppermute x1, waiting for transfers between devices, on_device(): moved_blocks = lax.ppermute(a_blocks, ('row', 'col'), to_b)  13.9 us
    pallas_call x1, Pallas kernels, run_first(): pl.pallas_call(functools.partial(first_kernel, bs, layers), name='first_p...  9.82 us
    ppermute x1, starting transfers between devices, on_device(): back_bound = lax.ppermute(bound, 'col', to_last)  9.22 us
    ppermute x1, waiting for transfers between devices, on_device(): moved_peak = lax.ppermute(peaks[:1], ('row', 'col'), to_b)  4.59 us
    ppermute x1, starting transfers between devices, on_device(): moved_blocks = lax.ppermute(a_blocks, ('row', 'col'), to_b)  4.54 us
    pallas_call x1, Pallas kernels, run_head(): pl.pallas_call(functools.partial(head_kernel, bs, layers), name='head_pro...  3.58 us
    pallas_call x2, Pallas kernels, scatter_blocks(): pl.pallas_call(scatter_kernel, name='scatter_blocks', out_shape=shape, in...  2.79 us
    ppermute x2, starting transfers between devices, on_device(): moved_slots = lax.ppermute((a_cells, a_count), ('row', 'col'), to_b)  2.65 us
  transfers between devices with their start and end apart: 12, of which 6 were waited for; matrix products, arithmetic and copies ran while one was open for 5% of the time, Pallas kernels for 5%

profile of v3, /device:TPU:0, one launch (start us, length us, event | category | flops | bytes accessed | tf_op | source)
XLA Modules:
  0.0 73.6 jit_solution(14837871041273332580)
XLA Ops:
  0.0 0.5 broadcast.73
  0.5 1.3 %reduce.5 = s32[32]{0:T(128)S(1)} reduce(s32[1,1,32]{2,1,0:T(1,128)} %param.13, s32[]{:T(128)} %broadcast.73), dimensions={0,1}, to_apply=%param.13.reduce_sub_computation.5 | reduce | bytes 260 | tf_op args[6]
  1.8 0.1 reshape_squeeze.3
  1.9 0.2 convert_reduce_fusion
  2.1 0.7 %stack_reshape_squeeze.3 = s32[1,2,16]{2,1,0:T(2,128)S(1)} reshape(s32[32]{0:T(128)} %bitcast.19) | data formatting | bytes 256 | tf_op jit(solution)/shard_map/stack;reshape;squeeze | solution.py:250
  2.9 0.1 select_reduce_fusion
  3.0 0.1 unstack.15.cells
  4.4 0.0 copy-start
  4.4 0.6 copy-done
  5.1 0.7 copy-done.1
  5.7 9.8 %first_product.1 = (f32[16,128,128]{2,1,0:T(8,128)S(1)}, f32[16,128,128]{2,1,0:T(8,128)S(1)}, bf16[8,1024,256]{2,1,0:T(8,128)(2,1)S(1)}, f32[2]{0:T(128)S(1)}) custom-call(s32[24]{0:T(128)S(1)} %bitcast.14, s32[1]{0:T(128)} %bitcast.11.a_count, s32[80]{0:T(128)S(1)} %bitcast.13, s32[1]{0:T(128)} %bitcast.12.b_count, s32[32]{0:T(128)S(1)} %unstack.15.cells, ...), custom_call_target="tpu_custom_call" | custom-call | flops 2147483648 | bytes 12582912 | tf_op jit(solution)/shard_map/first_product/pallas_call | solution.py:174
  15.6 0.6 collective-permute-start.1
  16.2 4.5 %collective-permute-start = (bf16[24,128,128]{2,1,0:T(8,128)(2,1)S(1)}, bf16[24,128,128]{2,1,0:T(8,128)(2,1)S(1)}, u32[]{:S(2)}, u32[]{:S(2)}) collective-permute-start(bf16[24,128,128]{2,1,0:T(8,128)(2,1)S(1)} %bitcast.18), channel_id=1, source_target_pairs={{8,2},{10,4},{12,6},{14,0},{16,10},{18,12},{20,14},{22,8},{24,18},... | collective-permute-start | bytes 2359304 | tf_op jit(solution)/shard_map/ppermute | solution.py:282
  20.7 1.3 %collective-permute-start.3 = (s32[32]{0:T(128)S(1)}, s32[32]{0:T(128)S(1)}, u32[]{:S(2)}, u32[]{:S(2)}) collective-permute-start(s32[32]{0:T(128)S(1)} %unstack.15.cells), channel_id=1, source_target_pairs={{0,2},{2,4},{4,6},{6,0},{1,3},{3,5},{5,7},{7,1},{8,10},{10,12},{12... | collective-permute-start | bytes 392 | tf_op jit(solution)/shard_map/ppermute | solution.py:288
  22.1 1.8 %collective-permute-start.4 = (s32[24]{0:T(128)S(1)}, s32[24]{0:T(128)S(1)}, u32[]{:S(2)}, u32[]{:S(2)}) collective-permute-start(s32[24]{0:T(128)S(1)} %bitcast.15), channel_id=1, source_target_pairs={{8,2},{10,4},{12,6},{14,0},{16,10},{18,12},{20,14},{22,8},{24,18},... | collective-permute-start | bytes 296 | tf_op jit(solution)/shard_map/ppermute | solution.py:283
  23.9 0.0 collective-permute-start.2
  23.9 1.2 %collective-permute-done.2 = f32[2]{0:T(128)S(1)} collective-permute-done((f32[2]{0:T(128)S(1)}, f32[2]{0:T(128)S(1)}, u32[]{:S(2)}, u32[]{:S(2)}) %collective-permute-start.2) | collective-permute-done | bytes 40 | tf_op jit(solution)/shard_map/ppermute | solution.py:258
  25.0 0.9 %collective-permute-start.5 = (s32[1]{0:T(128)}, s32[1]{0:T(128)}, u32[]{:S(2)}, u32[]{:S(2)}) collective-permute-start(s32[1]{0:T(128)} %bitcast.2), channel_id=1, source_target_pairs={{8,2},{10,4},{12,6},{14,0},{16,10},{18,12},{20,14},{22,8},{24,18},... | collective-permute-start | bytes 20 | tf_op jit(solution)/shard_map/ppermute | solution.py:283
  25.9 0.0 collective-permute-done.1
  25.9 0.1 add.52
  26.0 13.9 %collective-permute-done.a_blocks = bf16[24,128,128]{2,1,0:T(8,128)(2,1)S(1)} collective-permute-done((bf16[24,128,128]{2,1,0:T(8,128)(2,1)S(1)}, bf16[24,128,128]{2,1,0:T(8,128)(2,1)S(1)}, u32[]{:S(2)}, u32[]{:S(2)}) %collective-permute-start) | collective-permute-done | bytes 786464 | tf_op jit(solution)/shard_map/ppermute | solution.py:282
  40.0 0.2 collective-permute-done.5.a_count
  40.2 0.0 collective-permute-done.4.a_cells
  40.2 0.6 collective-permute-done.3.cells
  40.8 3.6 %head_product.1 = (f32[8,128,128]{2,1,0:T(8,128)S(1)}, f32[8,128,128]{2,1,0:T(8,128)S(1)}, bf16[512,1024]{1,0:T(8,128)(2,1)S(1)}, f32[16,4,128,128]{3,2,1,0:T(8,128)S(1)}) custom-call(s32[24]{0:T(128)S(1)} %collective-permute-done.4.a_cells, s32[1]{0:T(128)} %collective-permute-done.5.a_count, s32[32]{0:T(128)S(1)} %collective-permute-done.3.cells, ...), custom_call_target="tpu_custom_call" | custom-call | flops 1073741824 | bytes 4194304 | tf_op jit(solution)/shard_map/head_product/pallas_call | solution.py:199
  44.4 0.1 collective-permute-start.9
  44.4 2.5 %tail_product.1 = (f32[8,128,128]{2,1,0:T(8,128)S(1)}, f32[8,128,128]{2,1,0:T(8,128)S(1)}, f32[16,4,128,128]{3,2,1,0:T(8,128)S(1)}) custom-call(s32[32]{0:T(128)S(1)} %collective-permute-done.3.cells, s32[1]{0:T(128)} %bitcast.5.rot, bf16[512,1024]{1,0:T(8,128)(2,1)S(1)} %get-tuple-element.26.left, ...), custom_call_target="tpu_custom_call", output_to_operand_aliasing={{2}: (4, {})} | custom-call | flops 1073741824 | bytes 4194304 | tf_op jit(solution)/shard_map/tail_product/pallas_call | solution.py:215
  46.9 0.6 collective-permute-start.6
  47.5 0.1 unstack.13
  47.5 0.1 dynamic_slice.3
  47.6 0.6 fusion.5
  48.2 1.8 %collective-permute-start.7 = (f32[1]{0:T(128)}, f32[1]{0:T(128)}, u32[]{:S(2)}, u32[]{:S(2)}) collective-permute-start(f32[1]{0:T(128)} %get-tuple-element.40), channel_id=1, source_target_pairs={{8,2},{10,4},{12,6},{14,0},{16,10},{18,12},{20,14},{22,8},{24,18},... | collective-permute-start | bytes 20 | tf_op jit(solution)/shard_map/ppermute | solution.py:303
  50.1 4.6 %collective-permute-done.7 = f32[1]{0:T(128)} collective-permute-done((f32[1]{0:T(128)}, f32[1]{0:T(128)}, u32[]{:S(2)}, u32[]{:S(2)}) %collective-permute-start.7) | collective-permute-done | bytes 36 | tf_op jit(solution)/shard_map/ppermute | solution.py:303
  55.9 0.0 collective-permute-done.9
  55.9 1.2 %reduce-precision_convert_fusion = f16[8,128,128]{2,1,0:T(8,128)(2,1)S(1)} fusion(f32[8,128,128]{2,1,0:T(8,128)S(1)} %get-tuple-element.31, f32[8,128,128]{2,1,0:T(8,128)} %collective-permute-done.9, f32[]{:T(128)} %bitcast.7), kind=kLoop, calls=%fused_computation.2 | loop fusion | flops 524288 | bytes 1310724 | tf_op jit(solution)/shard_map/convert_element_type | solution.py:263
  57.2 0.7 %collective-permute-start.10 = (f16[8,128,128]{2,1,0:T(8,128)(2,1)S(1)}, f16[8,128,128]{2,1,0:T(8,128)(2,1)S(1)}, u32[]{:S(2)}, u32[]{:S(2)}) collective-permute-start(f16[8,128,128]{2,1,0:T(8,128)(2,1)S(1)} %reduce-precision_convert_fusion), channel_id=1, source_target_pairs={{0,6},{2,0},{4,2},{6,4},{1,7},{3,1},{5,3},{7,5},{8,14},{10,8},{12,... | collective-permute-start | bytes 786440 | tf_op jit(solution)/shard_map/ppermute | solution.py:307
  57.9 0.0 collective-permute-done.6
  57.9 1.2 %reduce-precision_convert_fusion.1 = f16[8,128,128]{2,1,0:T(8,128)(2,1)S(1)} fusion(f32[8,128,128]{2,1,0:T(8,128)S(1)} %get-tuple-element.28, f32[8,128,128]{2,1,0:T(8,128)} %collective-permute-done.6, f32[]{:T(128)} %bitcast.7), kind=kLoop, calls=%fused_computation.3 | loop fusion | flops 524288 | bytes 1310724 | tf_op jit(solution)/shard_map/convert_element_type | solution.py:263
  59.1 0.2 collective-permute-start.8
  59.3 0.1 fusion.4
  59.4 9.2 %collective-permute-start.11 = (f32[1]{0:T(128)}, f32[1]{0:T(128)}, u32[]{:S(2)}, u32[]{:S(2)}) collective-permute-start(f32[1]{0:T(128)} %max.7), channel_id=1, source_target_pairs={{0,6},{2,0},{4,2},{6,4},{1,7},{3,1},{5,3},{7,5},{8,14},{10,8},{12,... | collective-permute-start | bytes 20 | tf_op jit(solution)/shard_map/ppermute | solution.py:308
  68.6 1.4 %collective-permute-done.11 = f32[1]{0:T(128)} collective-permute-done((f32[1]{0:T(128)}, f32[1]{0:T(128)}, u32[]{:S(2)}, u32[]{:S(2)}) %collective-permute-start.11) | collective-permute-done | bytes 36 | tf_op jit(solution)/shard_map/ppermute | solution.py:308
  70.7 0.0 collective-permute-done.10
  70.7 0.1 multiply_add_fusion.1.blocks
  70.7 1.4 %scatter_blocks.2.refs_0_ = f32[16,128,128]{2,1,0:T(8,128)} custom-call(s32[8]{0:T(128)S(1)} %get-tuple-element.37.places, f32[8,128,128]{2,1,0:T(8,128)S(1)} %multiply_add_fusion.1.blocks), custom_call_target="tpu_custom_call" | custom-call | tf_op jit(solution)/shard_map/scatter_blocks/pallas_call | solution.py:231
  72.1 0.0 collective-permute-done.8
  72.2 0.1 multiply_add_fusion.blocks
  72.2 1.4 %scatter_blocks.3 = f32[16,128,128]{2,1,0:T(8,128)} custom-call(s32[8]{0:T(128)S(1)} %get-tuple-element.38.places, f32[8,128,128]{2,1,0:T(8,128)S(1)} %multiply_add_fusion.blocks, f32[16,128,128]{2,1,0:T(8,128)} %scatter_blocks.2.refs_0_), custom_call_target="tpu_custom_call", output_to_operand_aliasing={{}: (2, {})} | custom-call | tf_op jit(solution)/shard_map/scatter_blocks/pallas_call | solution.py:231
  (9 shorter events, 0.0 us)
Async XLA Ops:
  4.4 0.7 copy-start
  5.1 0.7 copy-start.1
  5.7 10.5 %copy-start.2 = (bf16[1,1,1,24,128,128]{5,4,3,2,1,0:T(8,128)(2,1)S(1)}, bf16[1,1,1,24,128,128]{5,4,3,2,1,0:T(8,128)(2,1)}, u32[]{:S(2)}) copy-start(bf16[1,1,1,24,128,128]{5,4,3,2,1,0:T(8,128)(2,1)} %param.7) | copy-start | bytes 2359300
  15.6 10.3 %collective-permute-start.1 = (f32[16,128,128]{2,1,0:T(8,128)S(1)}, f32[16,128,128]{2,1,0:T(8,128)S(1)}, u32[]{:S(2)}, u32[]{:S(2)}) collective-permute-start(f32[16,128,128]{2,1,0:T(8,128)S(1)} %get-tuple-element.21), channel_id=1, source_target_pairs={{0,1},{1,0},{2,3},{3,2},{4,5},{5,4},{6,7},{7,6},{8,9},{9,8},{10,11... | collective-permute-start | bytes 3145736 | tf_op jit(solution)/shard_map/ppermute | solution.py:258
  16.2 23.8 %collective-permute-start = (bf16[24,128,128]{2,1,0:T(8,128)(2,1)S(1)}, bf16[24,128,128]{2,1,0:T(8,128)(2,1)S(1)}, u32[]{:S(2)}, u32[]{:S(2)}) collective-permute-start(bf16[24,128,128]{2,1,0:T(8,128)(2,1)S(1)} %bitcast.18), channel_id=1, source_target_pairs={{8,2},{10,4},{12,6},{14,0},{16,10},{18,12},{20,14},{22,8},{24,18},... | collective-permute-start | bytes 2359304 | tf_op jit(solution)/shard_map/ppermute | solution.py:282
  20.7 20.0 %collective-permute-start.3 = (s32[32]{0:T(128)S(1)}, s32[32]{0:T(128)S(1)}, u32[]{:S(2)}, u32[]{:S(2)}) collective-permute-start(s32[32]{0:T(128)S(1)} %unstack.15.cells), channel_id=1, source_target_pairs={{0,2},{2,4},{4,6},{6,0},{1,3},{3,5},{5,7},{7,1},{8,10},{10,12},{12... | collective-permute-start | bytes 392 | tf_op jit(solution)/shard_map/ppermute | solution.py:288
  22.1 18.1 %collective-permute-start.4 = (s32[24]{0:T(128)S(1)}, s32[24]{0:T(128)S(1)}, u32[]{:S(2)}, u32[]{:S(2)}) collective-permute-start(s32[24]{0:T(128)S(1)} %bitcast.15), channel_id=1, source_target_pairs={{8,2},{10,4},{12,6},{14,0},{16,10},{18,12},{20,14},{22,8},{24,18},... | collective-permute-start | bytes 296 | tf_op jit(solution)/shard_map/ppermute | solution.py:283
  23.9 1.2 %collective-permute-start.2 = (f32[2]{0:T(128)S(1)}, f32[2]{0:T(128)S(1)}, u32[]{:S(2)}, u32[]{:S(2)}) collective-permute-start(f32[2]{0:T(128)S(1)} %get-tuple-element.22), channel_id=1, source_target_pairs={{0,1},{1,0},{2,3},{3,2},{4,5},{5,4},{6,7},{7,6},{8,9},{9,8},{10,11... | collective-permute-start | bytes 32 | tf_op jit(solution)/shard_map/ppermute | solution.py:258
  25.0 15.1 %collective-permute-start.5 = (s32[1]{0:T(128)}, s32[1]{0:T(128)}, u32[]{:S(2)}, u32[]{:S(2)}) collective-permute-start(s32[1]{0:T(128)} %bitcast.2), channel_id=1, source_target_pairs={{8,2},{10,4},{12,6},{14,0},{16,10},{18,12},{20,14},{22,8},{24,18},... | collective-permute-start | bytes 20 | tf_op jit(solution)/shard_map/ppermute | solution.py:283
  44.4 11.6 %collective-permute-start.9 = (f32[8,128,128]{2,1,0:T(8,128)S(1)}, f32[8,128,128]{2,1,0:T(8,128)}, u32[]{:S(2)}, u32[]{:S(2)}) collective-permute-start(f32[8,128,128]{2,1,0:T(8,128)S(1)} %get-tuple-element.32), channel_id=1, source_target_pairs={{0,1},{1,0},{2,3},{3,2},{4,5},{5,4},{6,7},{7,6},{8,9},{9,8},{10,11... | collective-permute-start | bytes 1572872 | tf_op jit(solution)/shard_map/ppermute | solution.py:258
  46.9 11.0 %collective-permute-start.6 = (f32[8,128,128]{2,1,0:T(8,128)S(1)}, f32[8,128,128]{2,1,0:T(8,128)}, u32[]{:S(2)}, u32[]{:S(2)}) collective-permute-start(f32[8,128,128]{2,1,0:T(8,128)S(1)} %get-tuple-element.29), channel_id=1, source_target_pairs={{0,1},{1,0},{2,3},{3,2},{4,5},{5,4},{6,7},{7,6},{8,9},{9,8},{10,11... | collective-permute-start | bytes 1572872 | tf_op jit(solution)/shard_map/ppermute | solution.py:258
  48.2 6.4 %collective-permute-start.7 = (f32[1]{0:T(128)}, f32[1]{0:T(128)}, u32[]{:S(2)}, u32[]{:S(2)}) collective-permute-start(f32[1]{0:T(128)} %get-tuple-element.40), channel_id=1, source_target_pairs={{8,2},{10,4},{12,6},{14,0},{16,10},{18,12},{20,14},{22,8},{24,18},... | collective-permute-start | bytes 20 | tf_op jit(solution)/shard_map/ppermute | solution.py:303
  57.2 13.5 %collective-permute-start.10 = (f16[8,128,128]{2,1,0:T(8,128)(2,1)S(1)}, f16[8,128,128]{2,1,0:T(8,128)(2,1)S(1)}, u32[]{:S(2)}, u32[]{:S(2)}) collective-permute-start(f16[8,128,128]{2,1,0:T(8,128)(2,1)S(1)} %reduce-precision_convert_fusion), channel_id=1, source_target_pairs={{0,6},{2,0},{4,2},{6,4},{1,7},{3,1},{5,3},{7,5},{8,14},{10,8},{12,... | collective-permute-start | bytes 786440 | tf_op jit(solution)/shard_map/ppermute | solution.py:307
  59.1 13.0 %collective-permute-start.8 = (f16[8,128,128]{2,1,0:T(8,128)(2,1)S(1)}, f16[8,128,128]{2,1,0:T(8,128)(2,1)S(1)}, u32[]{:S(2)}, u32[]{:S(2)}) collective-permute-start(f16[8,128,128]{2,1,0:T(8,128)(2,1)S(1)} %reduce-precision_convert_fusion.1), channel_id=1, source_target_pairs={{0,6},{2,0},{4,2},{6,4},{1,7},{3,1},{5,3},{7,5},{8,14},{10,8},{12,... | collective-permute-start | bytes 786440 | tf_op jit(solution)/shard_map/ppermute | solution.py:311
  59.4 10.6 %collective-permute-start.11 = (f32[1]{0:T(128)}, f32[1]{0:T(128)}, u32[]{:S(2)}, u32[]{:S(2)}) collective-permute-start(f32[1]{0:T(128)} %max.7), channel_id=1, source_target_pairs={{0,6},{2,0},{4,2},{6,4},{1,7},{3,1},{5,3},{7,5},{8,14},{10,8},{12,... | collective-permute-start | bytes 20 | tf_op jit(solution)/shard_map/ppermute | solution.py:308

commit v4 on v0

v4 whole, which is shorter than its diff:
```python
import functools

import jax
import jax.numpy as jnp
from jax import lax
from jax.experimental import pallas as pl
from jax.experimental.pallas import tpu as pltpu
from jax.sharding import PartitionSpec as P


CR = 4
CC = 16
KW = 8
PAIR = 2
GROUPS = CC // PAIR
F16_EXPONENT = 14.0
NOTE_ROWS = 16

HBM = pl.BlockSpec(memory_space=pltpu.HBM)
SMEM = pl.BlockSpec(memory_space=pltpu.SMEM)
VMEM = pl.BlockSpec(memory_space=pltpu.VMEM)


def left_cell(left, cell, bs):
    start = pl.multiple_of((cell % KW) * bs, bs)
    return left.at[pl.ds((cell // KW) * bs, bs), pl.ds(start, bs)]


def right_cell(right, cell, bs):
    panel, inner, col = cell // (KW * CC), (cell // CC) % KW, cell % CC
    start = pl.multiple_of((col % PAIR) * bs, bs)
    group = panel * GROUPS + col // PAIR
    return right.at[group, pl.ds(pl.multiple_of(inner * bs, bs), bs), pl.ds(start, bs)]


def place_slots(blocks, cell_list, count, cells, cell_ref, sem):
    @pl.loop(0, blocks.shape[0])
    def _(slot):
        cell = jnp.where(slot < count[0], cell_list[slot], cells + slot)
        pltpu.make_async_copy(blocks.at[slot], cell_ref(cell), sem).start()


def multiply(left, right, acc, group, bs):
    product = jnp.dot(left[...], right[group], preferred_element_type=jnp.float32)
    for half in range(PAIR):
        for row in range(CR):
            acc[group * PAIR + half, row] = product[
                row * bs : (row + 1) * bs, half * bs : (half + 1) * bs
            ]


def put_kept(kept, rot, acc, outs, bs):
    total = kept.shape[0]
    share = total // len(outs)
    for step, out in enumerate(outs):
        for place in range(share):
            cell = kept[lax.rem(step * share + place + rot[0], total)]
            out[place * bs : (place + 1) * bs] = acc[cell % CC, cell // CC]
        if out.shape[0] > share * bs:
            out[share * bs :] = jnp.zeros((out.shape[0] - share * bs, bs), out.dtype)


def first_kernel(bs, layers, a_cells, a_count, b_cells, b_count, kept, rot, a_blocks, b_blocks, *refs):
    outs, dense = refs[:layers], refs[layers]
    left, acc, a_sem, b_sem = refs[layers + 1 :]

    @pl.loop(0, GROUPS)
    def _(group):
        dense[group] = jnp.zeros(dense.shape[1:], dense.dtype)

    left[...] = jnp.zeros(left.shape, left.dtype)
    place_slots(
        b_blocks, b_cells, b_count, KW * CC, lambda cell: right_cell(dense, cell, bs), b_sem
    )
    place_slots(a_blocks, a_cells, a_count, CR * KW, lambda cell: left_cell(left, cell, bs), a_sem)
    pltpu.make_async_copy(b_blocks, b_blocks, b_sem).wait()
    pltpu.make_async_copy(a_blocks, a_blocks, a_sem).wait()

    @pl.loop(0, GROUPS)
    def _(group):
        multiply(left.at[pl.ds(0, CR * bs)], dense, acc, group, bs)

    put_kept(kept, rot, acc, outs, bs)


def second_kernel(bs, layers, a_cells, a_count, kept, rot, a_blocks, dense, *refs):
    outs, (left, acc, a_slot) = refs[:layers], refs[layers:]
    for cell in range(CR * KW):
        a_slot[cell] = -1

    @pl.loop(0, a_count[0])
    def _(slot):
        a_slot[a_cells[slot]] = slot

    for cell in range(CR * KW):
        slot = a_slot[cell]
        block = a_blocks[jnp.maximum(slot, 0)]
        left_cell(left, cell, bs)[...] = jnp.where(slot >= 0, block, jnp.zeros_like(block))

    @pl.loop(0, GROUPS)
    def _(group):
        multiply(left, dense, acc, group, bs)

    put_kept(kept, rot, acc, outs, bs)


def cost(bytes_accessed, bs):
    flops = 2 * CR * KW * CC * bs**3
    return pl.CostEstimate(flops=flops, bytes_accessed=bytes_accessed, transcendentals=0)


def run_first(layers, a_cells, a_count, b_cells, b_count, kept, rot, a_blocks, b_blocks):
    bs = a_blocks.shape[-1]
    spare_a, spare_b = pl.cdiv(a_blocks.shape[0], KW), pl.cdiv(b_blocks.shape[0], KW * CC)
    share = jax.ShapeDtypeStruct((kept.shape[0] // layers * bs, bs), jnp.float32)
    dense = jax.ShapeDtypeStruct(((1 + spare_b) * GROUPS, KW * bs, PAIR * bs), b_blocks.dtype)
    *outs, dense = pl.pallas_call(
        functools.partial(first_kernel, bs, layers),
        name="first_product",
        out_shape=[share] * layers + [dense],
        in_specs=[SMEM] * 6 + [HBM] * 2,
        out_specs=[VMEM] * (layers + 1),
        scratch_shapes=[
            pltpu.VMEM(((CR + spare_a) * bs, KW * bs), a_blocks.dtype),
            pltpu.VMEM((CC, CR, bs, bs), jnp.float32),
            pltpu.SemaphoreType.DMA,
            pltpu.SemaphoreType.DMA,
        ],
        compiler_params=pltpu.CompilerParams(vmem_limit_bytes=24 << 20),
        cost_estimate=cost(12 << 20, bs),
    )(a_cells, a_count, b_cells, b_count, kept, rot, a_blocks, b_blocks)
    return outs, dense


def run_second(layers, a_cells, a_count, kept, rot, a_blocks, dense):
    bs = a_blocks.shape[-1]
    share = jax.ShapeDtypeStruct((kept.shape[0] // layers * bs + NOTE_ROWS, bs), jnp.float32)
    return pl.pallas_call(
        functools.partial(second_kernel, bs, layers),
        name="second_product",
        out_shape=[share] * layers,
        in_specs=[SMEM] * 4 + [VMEM] * 2,
        out_specs=[VMEM] * layers,
        scratch_shapes=[
            pltpu.VMEM((CR * bs, KW * bs), a_blocks.dtype),
            pltpu.VMEM((CC, CR, bs, bs), jnp.float32),
            pltpu.SMEM((CR * KW,), jnp.int32),
        ],
        compiler_params=pltpu.CompilerParams(vmem_limit_bytes=24 << 20),
        cost_estimate=cost(8 << 20, bs),
    )(a_cells, a_count, kept, rot, a_blocks, dense)


def over_layers(combine, values, layers):
    total = values[0]
    for step in range(1, layers):
        perm = [(i, (i + step) % layers) for i in range(layers)]
        total = combine(total, lax.ppermute(values[step], "layer", perm))
    return total


def narrow(value):
    top = jnp.maximum(jnp.max(jnp.abs(value)), 1e-30)
    exponent = jnp.ceil(jnp.log2(top))
    rows = lax.broadcasted_iota(jnp.int32, value.shape, 0)
    scaled = value * jnp.exp2(F16_EXPONENT - exponent)
    return jnp.where(rows < value.shape[0] - NOTE_ROWS, scaled, exponent).astype(jnp.float16)


def widen(sent):
    exponent = sent[-NOTE_ROWS:][:1].astype(jnp.float32)
    return sent[:-NOTE_ROWS].astype(jnp.float32) * jnp.exp2(exponent - F16_EXPONENT)


def on_device(rows, cols, layers, a_blocks, a_cells, a_count, b_blocks, b_cells, b_count, c_cells):
    a_blocks, a_cells, a_count = a_blocks[0, 0, 0], a_cells[0, 0, 0], a_count[0, 0]
    b_blocks, b_cells, b_count = b_blocks[0, 0, 0], b_cells[0, 0, 0], b_count[0, 0]
    kept = c_cells.reshape(-1)
    to_b = [
        (((r + 1) % rows) * cols + c, r * cols + (c + 1) % cols)
        for r in range(rows)
        for c in range(cols)
    ]
    to_next = [(c, (c + 1) % cols) for c in range(cols)]
    to_last = [(c, (c - 1) % cols) for c in range(cols)]
    share, bs = kept.shape[0] // layers, a_blocks.shape[-1]
    rot = (lax.axis_index("layer").astype(jnp.int32) * share).reshape(1)

    moved_blocks = lax.ppermute(a_blocks, ("row", "col"), to_b)
    moved_cells, moved_count = lax.ppermute((a_cells, a_count), ("row", "col"), to_b)
    moved_kept = lax.ppermute(kept, "col", to_next)
    first, dense = run_first(
        layers,
        a_cells,
        a_count,
        b_cells,
        b_count,
        kept,
        rot,
        pltpu.with_memory_space_constraint(a_blocks, pltpu.HBM),
        pltpu.with_memory_space_constraint(b_blocks, pltpu.HBM),
    )
    second = run_second(layers, moved_cells, moved_count, moved_kept, rot, moved_blocks, dense)
    other = over_layers(jnp.add, second, layers)
    back = lax.ppermute(narrow(other), "col", to_last)
    own = over_layers(jnp.add, first, layers)
    total = own + widen(back)
    return total.reshape(1, 1, share, bs, bs)


def solution(mesh):
    sizes = mesh.shape
    return jax.shard_map(
        functools.partial(on_device, sizes["row"], sizes["col"], sizes["layer"]),
        mesh=mesh,
        in_specs=(
            P("row", "col", "layer", None, None, None),
            P("row", "col", "layer", None),
            P("row", "col", "layer"),
            P("row", "col", "layer", None, None, None),
            P("row", "col", "layer", None),
            P("row", "col", "layer"),
            P("row", "col", None),
        ),
        out_specs=P("row", "col", "layer", None, None),
        check_vma=False,
    )
```

time: 122 us -> 51.6 us (0.42)
  local copies, waits for them, and re-layouts: 35.5 us -> 1.96 us
  matrix products: 17.9 us -> 0 us
  Pallas kernels: 0 us -> 13.9 us
  between operations: 14.9 us -> 2.08 us
  other arithmetic: 14 us -> 3.45 us
  waiting for transfers between devices: 28.5 us -> 18.3 us
    gather x8 -> x0, local copies, waits for them, and re-layouts: 35.5 us -> none  [the longest x2 14.4 us: kept_product(): right_cols = jnp.take(right, kept_cols, axis=1)]
    dot_general x2 -> x0, matrix products: 17.9 us -> none  [kept_product(): jnp.einsum('tkxz,ktzy->txy', left_rows, right_cols, preferred_element_typ...]
    pallas_call x0 -> x2, Pallas kernels: none -> 13.9 us  [the longest x1 8.38 us: run_first(): pl.pallas_call(functools.partial(first_kernel, bs, layers), name='first_p...]
    reduce_scatter x1 -> x0, waiting for transfers between devices: 9.83 us -> none  [on_device(): lax.psum_scatter(both_stops, 'layer', scatter_dimension=0, tiled=True)]
    select_n x8 -> x0, other arithmetic: 8.59 us -> none  [the longest x4 8.57 us: densify(): jnp.where(present[:, None, None], picked, jnp.zeros((), blocks.dtype))]
    add x0 -> x1, other arithmetic: none -> 2.39 us  [on_device(): total = own + widen(back)]
    unnamed x2 -> x6, local copies, waits for them, and re-layouts: 0.01 us -> 1.96 us
    reduce_or x4 -> x0, other arithmetic: 1.71 us -> none  [densify(): present = jnp.any(matches, axis=1)]
  transfers between devices with their start and end apart: 7 -> 7, of which waited for: 3 -> 4; matrix products, arithmetic and copies ran while one was open for 28% -> 2% of each run, Pallas kernels for 0% -> 16%
where the time goes in v4:
time: 51.6 us; the launch traced here: 51.3 us
  waiting for transfers between devices  18.3 us (35%)
  Pallas kernels  13.9 us (27%)
  starting transfers between devices  11.6 us (22%)
  other arithmetic  3.45 us (7%)
  between operations  2.08 us (4%)
  local copies, waits for them, and re-layouts  1.96 us (4%)
    ppermute x1, waiting for transfers between devices, on_device(): back = lax.ppermute(narrow(other), 'col', to_last)  12.3 us
    pallas_call x1, Pallas kernels, run_first(): pl.pallas_call(functools.partial(first_kernel, bs, layers), name='first_p...  8.38 us
    pallas_call x1, Pallas kernels, run_second(): pl.pallas_call(functools.partial(second_kernel, bs, layers), name='second...  5.53 us
    ppermute x1, starting transfers between devices, on_device(): moved_blocks = lax.ppermute(a_blocks, ('row', 'col'), to_b)  4.94 us
    ppermute x2, starting transfers between devices, on_device(): lax.ppermute((a_cells, a_count), ('row', 'col'), to_b)  3.99 us
    ppermute x2, waiting for transfers between devices, on_device(): lax.ppermute((a_cells, a_count), ('row', 'col'), to_b)  3.17 us
    add x1, other arithmetic, on_device(): total = own + widen(back)  2.39 us
    ppermute x2, waiting for transfers between devices, over_layers(): total = combine(total, lax.ppermute(values[step], 'layer', perm))  2.16 us
  transfers between devices with their start and end apart: 7, of which 4 were waited for; matrix products, arithmetic and copies ran while one was open for 2% of the time, Pallas kernels for 16%

profile of v4, /device:TPU:0, one launch (start us, length us, event | category | flops | bytes accessed | tf_op | source)
XLA Modules:
  0.0 51.3 jit_solution(2672823535534837215)
XLA Ops:
  0.0 4.9 %collective-permute-start.4 = (bf16[24,128,128]{2,1,0:T(8,128)(2,1)}, bf16[24,128,128]{2,1,0:T(8,128)(2,1)S(1)}, u32[]{:S(2)}, u32[]{:S(2)}) collective-permute-start(bf16[24,128,128]{2,1,0:T(8,128)(2,1)} %bitcast.19), channel_id=1, source_target_pairs={{8,2},{10,4},{12,6},{14,0},{16,10},{18,12},{20,14},{22,8},{24,18},... | collective-permute-start | bytes 2359304 | tf_op jit(solution)/shard_map/ppermute | solution.py:189
  4.9 1.5 %collective-permute-start.1 = (s32[24]{0:T(128)}, s32[24]{0:T(128)S(1)}, u32[]{:S(2)}, u32[]{:S(2)}) collective-permute-start(s32[24]{0:T(128)} %bitcast.14), channel_id=1, source_target_pairs={{8,2},{10,4},{12,6},{14,0},{16,10},{18,12},{20,14},{22,8},{24,18},... | collective-permute-start | bytes 296 | tf_op jit(solution)/shard_map/ppermute | solution.py:190
  6.5 2.4 %collective-permute-start.2 = (s32[1]{0:T(128)}, s32[1]{0:T(128)}, u32[]{:S(2)}, u32[]{:S(2)}) collective-permute-start(s32[1]{0:T(128)} %bitcast.1), channel_id=1, source_target_pairs={{8,2},{10,4},{12,6},{14,0},{16,10},{18,12},{20,14},{22,8},{24,18},... | collective-permute-start | bytes 20 | tf_op jit(solution)/shard_map/ppermute | solution.py:190
  8.9 0.2 collective-permute-start.3
  10.5 0.0 copy-start
  10.5 0.6 %copy-done = s32[1,1,1,80]{3,2,1,0:T(1,128)S(1)} copy-done((s32[1,1,1,80]{3,2,1,0:T(1,128)S(1)}, s32[1,1,1,80]{3,2,1,0:T(1,128)}, u32[]{:S(2)}) %copy-start) | copy-done | bytes 344
  11.1 0.0 copy-start.1
  11.1 0.7 %copy-done.1 = s32[1,1,1,24]{3,2,1,0:T(1,128)S(1)} copy-done((s32[1,1,1,24]{3,2,1,0:T(1,128)S(1)}, s32[1,1,1,24]{3,2,1,0:T(1,128)}, u32[]{:S(2)}) %copy-start.1) | copy-done | bytes 120
  11.8 0.0 copy-start.2
  11.8 0.7 %copy-done.2 = s32[1,1,32]{2,1,0:T(1,128)S(1)} copy-done((s32[1,1,32]{2,1,0:T(1,128)S(1)}, s32[1,1,32]{2,1,0:T(1,128)}, u32[]{:S(2)}) %copy-start.2) | copy-done | bytes 152
  12.4 8.4 %first_product.1 = (f32[2048,128]{1,0:T(8,128)S(1)}, f32[2048,128]{1,0:T(8,128)S(1)}, bf16[16,1024,256]{2,1,0:T(8,128)(2,1)S(1)}) custom-call(s32[24]{0:T(128)S(1)} %bitcast.15, s32[1]{0:T(128)} %bitcast.11.a_count, s32[80]{0:T(128)S(1)} %bitcast.13, s32[1]{0:T(128)} %bitcast.12.b_count, s32[32]{0:T(128)S(1)} %bitcast.17, s32[1]{0:T(128)} %bitcast.5.rot, ...), custom_call_target="tpu_custom_call" | custom-call | flops 2147483648 | bytes 12582912 | tf_op jit(solution)/shard_map/first_product/pallas_call | solution.py:117
  20.8 3.2 %collective-permute-done.2.a_count = s32[1]{0:T(128)} collective-permute-done((s32[1]{0:T(128)}, s32[1]{0:T(128)}, u32[]{:S(2)}, u32[]{:S(2)}) %collective-permute-start.2) | collective-permute-done | bytes 36 | tf_op jit(solution)/shard_map/ppermute | solution.py:190
  24.0 0.0 collective-permute-done.1.a_cells
  24.0 0.7 %collective-permute-done.3.kept = s32[32]{0:T(128)S(1)} collective-permute-done((s32[32]{0:T(128)}, s32[32]{0:T(128)S(1)}, u32[]{:S(2)}, u32[]{:S(2)}) %collective-permute-start.3) | collective-permute-done | bytes 160 | tf_op jit(solution)/shard_map/ppermute | solution.py:191
  24.7 0.0 collective-permute-done.4.a_blocks
  24.7 5.5 %second_product.1 = (f32[2064,128]{1,0:T(8,128)S(1)}, f32[2064,128]{1,0:T(8,128)S(1)}) custom-call(s32[24]{0:T(128)S(1)} %collective-permute-done.1.a_cells, s32[1]{0:T(128)} %collective-permute-done.2.a_count, s32[32]{0:T(128)S(1)} %collective-permute-done.3.kept, s32[1]{0:T(128)} %bitcast.5.rot, bf16[24,128,128]{2,1,0:T(8,128)(2,1)S(1)} %collective-permute-done.4.a_blocks, ...), custom_call_target="tpu_custom_call" | custom-call | flops 2147483648 | bytes 8388608 | tf_op jit(solution)/shard_map/second_product/pallas_call | solution.py:138
  30.2 0.1 collective-permute-start.5
  30.3 0.5 collective-permute-start
  30.8 2.2 %collective-permute-done.5 = f32[2064,128]{1,0:T(8,128)S(1)} collective-permute-done((f32[2064,128]{1,0:T(8,128)S(1)}, f32[2064,128]{1,0:T(8,128)S(1)}, u32[]{:S(2)}, u32[]{:S(2)}) %collective-permute-start.5) | collective-permute-done | bytes 1056800 | tf_op jit(solution)/shard_map/ppermute | solution.py:158
  33.0 0.7 %abs_reduce_fusion = (f32[]{:T(128)}, f32[2064,128]{1,0:T(8,128)S(1)}) fusion(f32[2064,128]{1,0:T(8,128)S(1)} %get-tuple-element.13, f32[2064,128]{1,0:T(8,128)S(1)} %collective-permute-done.5), kind=kLoop, calls=%fused_computation.1 | loop fusion | flops 792575 | bytes 3170308 | tf_op jit(solution)/shard_map/reduce_max | solution.py:163
  34.4 0.3 select_convert_fusion
  34.8 1.8 %collective-permute-start.6 = (f16[2064,128]{1,0:T(8,128)(2,1)S(1)}, f16[2064,128]{1,0:T(8,128)(2,1)S(1)}, u32[]{:S(2)}, u32[]{:S(2)}) collective-permute-start(f16[2064,128]{1,0:T(8,128)(2,1)S(1)} %select_convert_fusion), channel_id=1, source_target_pairs={{0,6},{2,0},{4,2},{6,4},{1,7},{3,1},{5,3},{7,5},{8,14},{10,8},{12,... | collective-permute-start | bytes 1585160 | tf_op jit(solution)/shard_map/ppermute | solution.py:205
  36.6 12.3 %collective-permute-done.6 = f16[2064,128]{1,0:T(8,128)(2,1)S(1)} collective-permute-done((f16[2064,128]{1,0:T(8,128)(2,1)S(1)}, f16[2064,128]{1,0:T(8,128)(2,1)S(1)}, u32[]{:S(2)}, u32[]{:S(2)}) %collective-permute-start.6) | collective-permute-done | bytes 528416 | tf_op jit(solution)/shard_map/ppermute | solution.py:205
  48.9 0.0 collective-permute-done
  48.9 2.4 %multiply_add_fusion = f32[2048,128]{1,0:T(8,128)} fusion(f32[2048,128]{1,0:T(8,128)S(1)} %get-tuple-element.10, f32[2048,128]{1,0:T(8,128)} %collective-permute-done, f16[2064,128]{1,0:T(8,128)(2,1)S(1)} %collective-permute-done.6, f32[128]{0:T(128)S(1)} %fusion.3), kind=kLoop, calls=%fused_computation.2 | loop fusion | flops 1048576 | bytes 3670528 | tf_op jit(solution)/shard_map/add | solution.py:207
  (2 shorter events, 0.0 us)
Async XLA Ops:
  0.0 24.7 %collective-permute-start.4 = (bf16[24,128,128]{2,1,0:T(8,128)(2,1)}, bf16[24,128,128]{2,1,0:T(8,128)(2,1)S(1)}, u32[]{:S(2)}, u32[]{:S(2)}) collective-permute-start(bf16[24,128,128]{2,1,0:T(8,128)(2,1)} %bitcast.19), channel_id=1, source_target_pairs={{8,2},{10,4},{12,6},{14,0},{16,10},{18,12},{20,14},{22,8},{24,18},... | collective-permute-start | bytes 2359304 | tf_op jit(solution)/shard_map/ppermute | solution.py:189
  4.9 19.0 %collective-permute-start.1 = (s32[24]{0:T(128)}, s32[24]{0:T(128)S(1)}, u32[]{:S(2)}, u32[]{:S(2)}) collective-permute-start(s32[24]{0:T(128)} %bitcast.14), channel_id=1, source_target_pairs={{8,2},{10,4},{12,6},{14,0},{16,10},{18,12},{20,14},{22,8},{24,18},... | collective-permute-start | bytes 296 | tf_op jit(solution)/shard_map/ppermute | solution.py:190
  6.5 17.5 %collective-permute-start.2 = (s32[1]{0:T(128)}, s32[1]{0:T(128)}, u32[]{:S(2)}, u32[]{:S(2)}) collective-permute-start(s32[1]{0:T(128)} %bitcast.1), channel_id=1, source_target_pairs={{8,2},{10,4},{12,6},{14,0},{16,10},{18,12},{20,14},{22,8},{24,18},... | collective-permute-start | bytes 20 | tf_op jit(solution)/shard_map/ppermute | solution.py:190
  8.9 15.8 %collective-permute-start.3 = (s32[32]{0:T(128)}, s32[32]{0:T(128)S(1)}, u32[]{:S(2)}, u32[]{:S(2)}) collective-permute-start(s32[32]{0:T(128)} %bitcast.16), channel_id=1, source_target_pairs={{0,2},{2,4},{4,6},{6,0},{1,3},{3,5},{5,7},{7,1},{8,10},{10,12},{12... | collective-permute-start | bytes 392 | tf_op jit(solution)/shard_map/ppermute | solution.py:191
  10.5 0.7 %copy-start = (s32[1,1,1,80]{3,2,1,0:T(1,128)S(1)}, s32[1,1,1,80]{3,2,1,0:T(1,128)}, u32[]{:S(2)}) copy-start(s32[1,1,1,80]{3,2,1,0:T(1,128)} %param.11) | copy-start | bytes 964
  11.1 0.7 %copy-start.1 = (s32[1,1,1,24]{3,2,1,0:T(1,128)S(1)}, s32[1,1,1,24]{3,2,1,0:T(1,128)}, u32[]{:S(2)}) copy-start(s32[1,1,1,24]{3,2,1,0:T(1,128)} %param.8) | copy-start | bytes 292
  11.8 0.7 %copy-start.2 = (s32[1,1,32]{2,1,0:T(1,128)S(1)}, s32[1,1,32]{2,1,0:T(1,128)}, u32[]{:S(2)}) copy-start(s32[1,1,32]{2,1,0:T(1,128)} %param.13) | copy-start | bytes 388
  30.2 2.7 %collective-permute-start.5 = (f32[2064,128]{1,0:T(8,128)S(1)}, f32[2064,128]{1,0:T(8,128)S(1)}, u32[]{:S(2)}, u32[]{:S(2)}) collective-permute-start(f32[2064,128]{1,0:T(8,128)S(1)} %get-tuple-element.14), channel_id=1, source_target_pairs={{0,1},{1,0},{2,3},{3,2},{4,5},{5,4},{6,7},{7,6},{8,9},{9,8},{10,11... | collective-permute-start | bytes 3170312 | tf_op jit(solution)/shard_map/ppermute | solution.py:158
  30.3 18.6 %collective-permute-start = (f32[2048,128]{1,0:T(8,128)S(1)}, f32[2048,128]{1,0:T(8,128)}, u32[]{:S(2)}, u32[]{:S(2)}) collective-permute-start(f32[2048,128]{1,0:T(8,128)S(1)} %get-tuple-element.11), channel_id=1, source_target_pairs={{0,1},{1,0},{2,3},{3,2},{4,5},{5,4},{6,7},{7,6},{8,9},{9,8},{10,11... | collective-permute-start | bytes 3145736 | tf_op jit(solution)/shard_map/ppermute | solution.py:158
  34.8 14.1 %collective-permute-start.6 = (f16[2064,128]{1,0:T(8,128)(2,1)S(1)}, f16[2064,128]{1,0:T(8,128)(2,1)S(1)}, u32[]{:S(2)}, u32[]{:S(2)}) collective-permute-start(f16[2064,128]{1,0:T(8,128)(2,1)S(1)} %select_convert_fusion), channel_id=1, source_target_pairs={{0,6},{2,0},{4,2},{6,4},{1,7},{3,1},{5,3},{7,5},{8,14},{10,8},{12,... | collective-permute-start | bytes 1585160 | tf_op jit(solution)/shard_map/ppermute | solution.py:205

commit v5 on v4

v5 whole, which is shorter than its diff:
```python
import functools

import jax
import jax.numpy as jnp
from jax import lax
from jax.experimental import pallas as pl
from jax.experimental.pallas import tpu as pltpu
from jax.sharding import PartitionSpec as P


CR = 4
CC = 16
KW = 8
F16_EXPONENT = 14.0
NOTE_ROWS = 16

HBM = pl.BlockSpec(memory_space=pltpu.HBM)
SMEM = pl.BlockSpec(memory_space=pltpu.SMEM)
VMEM = pl.BlockSpec(memory_space=pltpu.VMEM)


def left_cell(left, cell, bs):
    start = pl.multiple_of((cell % KW) * bs, bs)
    return left.at[pl.ds((cell // KW) * bs, bs), pl.ds(start, bs)]


def right_cell(right, cell, bs):
    panel, inner, col = cell // (KW * CC), (cell // CC) % KW, cell % CC
    return right.at[panel * CC + col, pl.ds(pl.multiple_of(inner * bs, bs), bs)]


def place_slots(blocks, cell_list, count, cells, cell_ref, sem):
    @pl.loop(0, blocks.shape[0])
    def _(slot):
        cell = jnp.where(slot < count[0], cell_list[slot], cells + slot)
        pltpu.make_async_copy(blocks.at[slot], cell_ref(cell), sem).start()


def pair_up(kept, first, second, pending):
    for row in range(CR):
        pending[row] = -1
    count = 0
    for place in range(kept.shape[0]):
        row = kept[place] // CC
        waiting = pending[row]
        first[count], second[count] = waiting, place
        count = count + (waiting >= 0).astype(jnp.int32)
        pending[row] = jnp.where(waiting >= 0, -1, place)
    for row in range(CR):
        waiting = pending[row]
        first[count], second[count] = waiting, waiting
        count = count + (waiting >= 0).astype(jnp.int32)
    for spare in range(CR // 2):
        first[count + spare], second[count + spare] = first[0], second[0]


def pairs_of(capacity):
    return (capacity + CR) // 2


def multiply_kept(kept, rot, first, second, left, right, out, bs):
    total, layers = kept.shape[0], out.shape[0]
    share = total // layers
    top = jnp.zeros((8, bs), jnp.float32)
    for pair in range(pairs_of(total)):
        places = first[pair], second[pair]
        cells = [kept[place] for place in places]
        rows = left[pl.ds(pl.multiple_of((cells[0] // CC) * bs, bs), bs)]
        cols = jnp.concatenate([right[cell % CC] for cell in cells], axis=1)
        product = jnp.dot(rows, cols, preferred_element_type=jnp.float32)
        for half, place in enumerate(places):
            block = product[:, half * bs : (half + 1) * bs]
            to = lax.rem(place - rot[0] + total, total)
            start = pl.multiple_of((to % share) * bs, bs)
            out[to // share, pl.ds(start, bs)] = block
            top = jnp.maximum(top, jnp.max(jnp.abs(block).reshape(-1, 8, bs), axis=0))
    return top


def first_kernel(bs, a_cells, a_count, b_cells, b_count, kept, rot, a_blocks, b_blocks, *refs):
    out, dense, left, first, second, pending, a_sem, b_sem = refs

    @pl.loop(0, CC)
    def _(col):
        dense[col] = jnp.zeros(dense.shape[1:], dense.dtype)

    left[...] = jnp.zeros(left.shape, left.dtype)
    place_slots(
        b_blocks, b_cells, b_count, KW * CC, lambda cell: right_cell(dense, cell, bs), b_sem
    )
    place_slots(a_blocks, a_cells, a_count, CR * KW, lambda cell: left_cell(left, cell, bs), a_sem)
    pair_up(kept, first, second, pending)
    pltpu.make_async_copy(b_blocks, b_blocks, b_sem).wait()
    pltpu.make_async_copy(a_blocks, a_blocks, a_sem).wait()
    multiply_kept(kept, rot, first, second, left, dense, out, bs)


def second_kernel(bs, a_cells, a_count, kept, rot, a_blocks, dense, *refs):
    out, left, a_slot, first, second, pending = refs
    for cell in range(CR * KW):
        a_slot[cell] = -1

    @pl.loop(0, a_count[0])
    def _(slot):
        a_slot[a_cells[slot]] = slot

    pair_up(kept, first, second, pending)
    for cell in range(CR * KW):
        slot = a_slot[cell]
        block = a_blocks[jnp.maximum(slot, 0)]
        left_cell(left, cell, bs)[...] = jnp.where(slot >= 0, block, jnp.zeros_like(block))

    top = multiply_kept(kept, rot, first, second, left, dense, out, bs)
    for layer in range(out.shape[0]):
        for start in range(out.shape[1] - NOTE_ROWS, out.shape[1], 8):
            out[layer, start : start + 8] = top


def cost(bytes_accessed, bs):
    flops = CR * KW * CC * bs**3
    return pl.CostEstimate(flops=flops, bytes_accessed=bytes_accessed, transcendentals=0)


def pair_scratch(capacity):
    lists = pltpu.SMEM((pairs_of(capacity) + CR // 2,), jnp.int32)
    return [lists, lists, pltpu.SMEM((CR,), jnp.int32)]


def run_first(layers, a_cells, a_count, b_cells, b_count, kept, rot, a_blocks, b_blocks):
    bs = a_blocks.shape[-1]
    spare_a, spare_b = pl.cdiv(a_blocks.shape[0], KW), pl.cdiv(b_blocks.shape[0], KW * CC)
    return pl.pallas_call(
        functools.partial(first_kernel, bs),
        name="first_product",
        out_shape=[
            jax.ShapeDtypeStruct((layers, kept.shape[0] // layers * bs, bs), jnp.float32),
            jax.ShapeDtypeStruct(((1 + spare_b) * CC, KW * bs, bs), b_blocks.dtype),
        ],
        in_specs=[SMEM] * 6 + [HBM] * 2,
        out_specs=[VMEM] * 2,
        scratch_shapes=[pltpu.VMEM(((CR + spare_a) * bs, KW * bs), a_blocks.dtype)]
        + pair_scratch(kept.shape[0])
        + [pltpu.SemaphoreType.DMA] * 2,
        compiler_params=pltpu.CompilerParams(vmem_limit_bytes=20 << 20),
        cost_estimate=cost(12 << 20, bs),
    )(a_cells, a_count, b_cells, b_count, kept, rot, a_blocks, b_blocks)


def run_second(layers, a_cells, a_count, kept, rot, a_blocks, dense):
    bs = a_blocks.shape[-1]
    rows = kept.shape[0] // layers * bs + NOTE_ROWS
    return pl.pallas_call(
        functools.partial(second_kernel, bs),
        name="second_product",
        out_shape=jax.ShapeDtypeStruct((layers, rows, bs), jnp.float32),
        in_specs=[SMEM] * 4 + [VMEM] * 2,
        out_specs=VMEM,
        scratch_shapes=[
            pltpu.VMEM((CR * bs, KW * bs), a_blocks.dtype),
            pltpu.SMEM((CR * KW,), jnp.int32),
        ]
        + pair_scratch(kept.shape[0]),
        compiler_params=pltpu.CompilerParams(vmem_limit_bytes=20 << 20),
        cost_estimate=cost(8 << 20, bs),
    )(a_cells, a_count, kept, rot, a_blocks, dense)


def over_layers(combine, values, layers):
    total = values[0]
    for step in range(1, layers):
        perm = [(i, (i + step) % layers) for i in range(layers)]
        total = combine(total, lax.ppermute(values[step], "layer", perm))
    return total


def narrow(value):
    tiles = value.reshape(-1, 8, value.shape[-1])
    notes = NOTE_ROWS // 8
    exponent = jnp.ceil(jnp.log2(jnp.maximum(tiles[-1], 1e-30)))
    scaled = tiles[:-notes] * jnp.exp2(F16_EXPONENT - exponent)[None]
    noted = jnp.broadcast_to(exponent[None], (notes,) + exponent.shape)
    return jnp.concatenate([scaled, noted]).astype(jnp.float16).reshape(value.shape)


def widen(sent):
    tiles = sent.astype(jnp.float32).reshape(-1, 8, sent.shape[-1])
    scaled = tiles[: -(NOTE_ROWS // 8)] * jnp.exp2(tiles[-1] - F16_EXPONENT)[None]
    return scaled.reshape(-1, sent.shape[-1])


def on_device(rows, cols, layers, a_blocks, a_cells, a_count, b_blocks, b_cells, b_count, c_cells):
    a_blocks, a_cells, a_count = a_blocks[0, 0, 0], a_cells[0, 0, 0], a_count[0, 0]
    b_blocks, b_cells, b_count = b_blocks[0, 0, 0], b_cells[0, 0, 0], b_count[0, 0]
    kept = c_cells.reshape(-1)
    to_b = [
        (((r + 1) % rows) * cols + c, r * cols + (c + 1) % cols)
        for r in range(rows)
        for c in range(cols)
    ]
    to_next = [(c, (c + 1) % cols) for c in range(cols)]
    to_last = [(c, (c - 1) % cols) for c in range(cols)]
    share, bs = kept.shape[0] // layers, a_blocks.shape[-1]
    rot = (lax.axis_index("layer").astype(jnp.int32) * share).reshape(1)

    moved_blocks = lax.ppermute(a_blocks, ("row", "col"), to_b)
    moved_cells, moved_count = lax.ppermute((a_cells, a_count), ("row", "col"), to_b)
    moved_kept = lax.ppermute(kept, "col", to_next)
    first, dense = run_first(
        layers,
        a_cells,
        a_count,
        b_cells,
        b_count,
        kept,
        rot,
        pltpu.with_memory_space_constraint(a_blocks, pltpu.HBM),
        pltpu.with_memory_space_constraint(b_blocks, pltpu.HBM),
    )
    second = run_second(layers, moved_cells, moved_count, moved_kept, rot, moved_blocks, dense)
    other = over_layers(jnp.add, second, layers)
    back = lax.ppermute(narrow(other), "col", to_last)
    own = over_layers(jnp.add, first, layers)
    total = own + widen(back)
    return total.reshape(1, 1, share, bs, bs)


def solution(mesh):
    sizes = mesh.shape
    return jax.shard_map(
        functools.partial(on_device, sizes["row"], sizes["col"], sizes["layer"]),
        mesh=mesh,
        in_specs=(
            P("row", "col", "layer", None, None, None),
            P("row", "col", "layer", None),
            P("row", "col", "layer"),
            P("row", "col", "layer", None, None, None),
            P("row", "col", "layer", None),
            P("row", "col", "layer"),
            P("row", "col", None),
        ),
        out_specs=P("row", "col", "layer", None, None),
        check_vma=False,
    )
```

time: 51.6 us -> 47.1 us (0.913)
  Pallas kernels: 13.9 us -> 9.36 us
  waiting for transfers between devices: 18.3 us -> 20.7 us
  other arithmetic: 3.45 us -> 1.61 us
  between operations: 2.08 us -> 1.43 us
    pallas_call x2, Pallas kernels: 13.9 us -> 9.36 us  [the longest x1 5.8 us: run_first(): pl.pallas_call(functools.partial(first_kernel, bs), name='first_product',...]
    ppermute x2, waiting for transfers between devices: 3.17 us -> 5.6 us  [on_device(): lax.ppermute((a_cells, a_count), ('row', 'col'), to_b)]
    ppermute x2, starting transfers between devices: 3.99 us -> 2.64 us  [on_device(): lax.ppermute((a_cells, a_count), ('row', 'col'), to_b)]
    ppermute x1, starting transfers between devices: 0.22 us -> 1.58 us  [on_device(): moved_kept = lax.ppermute(kept, 'col', to_next)]
    add x1, other arithmetic: 2.39 us -> 1.12 us  [on_device(): total = own + widen(back)]
    reduce_max x1 -> x0, other arithmetic: 0.71 us -> none  [narrow(): top = jnp.maximum(jnp.max(jnp.abs(value)), 1e-30)]
  transfers between devices with their start and end apart: 7 -> 7, of which waited for: 4 -> 4; matrix products, arithmetic and copies ran while one was open for 2% -> 1% of each run, Pallas kernels for 16% -> 12%
where the time goes in v5:
time: 47.1 us; the launch traced here: 46.8 us
  waiting for transfers between devices  20.7 us (44%)
  starting transfers between devices  11.6 us (25%)
  Pallas kernels  9.36 us (20%)
  local copies, waits for them, and re-layouts  2.1 us (4%)
  other arithmetic  1.61 us (3%)
  between operations  1.43 us (3%)
    ppermute x1, waiting for transfers between devices, on_device(): back = lax.ppermute(narrow(other), 'col', to_last)  12.3 us
    pallas_call x1, Pallas kernels, run_first(): pl.pallas_call(functools.partial(first_kernel, bs), name='first_product',...  5.8 us
    ppermute x2, waiting for transfers between devices, on_device(): lax.ppermute((a_cells, a_count), ('row', 'col'), to_b)  5.6 us
    ppermute x1, starting transfers between devices, on_device(): moved_blocks = lax.ppermute(a_blocks, ('row', 'col'), to_b)  4.94 us
    pallas_call x1, Pallas kernels, run_second(): pl.pallas_call(functools.partial(second_kernel, bs), name='second_product...  3.57 us
    ppermute x2, starting transfers between devices, on_device(): lax.ppermute((a_cells, a_count), ('row', 'col'), to_b)  2.64 us
    ppermute x2, waiting for transfers between devices, over_layers(): total = combine(total, lax.ppermute(values[step], 'layer', perm))  2.03 us
    unnamed x6, local copies, waits for them, and re-layouts  1.96 us
  transfers between devices with their start and end apart: 7, of which 4 were waited for; matrix products, arithmetic and copies ran while one was open for 1% of the time, Pallas kernels for 12%

profile of v5, /device:TPU:0, one launch (start us, length us, event | category | flops | bytes accessed | tf_op | source)
XLA Modules:
  0.0 46.8 jit_solution(13973763389183994064)
XLA Ops:
  0.0 4.9 %collective-permute-start.4 = (bf16[24,128,128]{2,1,0:T(8,128)(2,1)}, bf16[24,128,128]{2,1,0:T(8,128)(2,1)S(1)}, u32[]{:S(2)}, u32[]{:S(2)}) collective-permute-start(bf16[24,128,128]{2,1,0:T(8,128)(2,1)} %bitcast.39), channel_id=1, source_target_pairs={{8,2},{10,4},{12,6},{14,0},{16,10},{18,12},{20,14},{22,8},{24,18},... | collective-permute-start | bytes 2359304 | tf_op jit(solution)/shard_map/ppermute | solution.py:205
  4.9 1.5 %collective-permute-start.1 = (s32[24]{0:T(128)}, s32[24]{0:T(128)S(1)}, u32[]{:S(2)}, u32[]{:S(2)}) collective-permute-start(s32[24]{0:T(128)} %bitcast.34), channel_id=1, source_target_pairs={{8,2},{10,4},{12,6},{14,0},{16,10},{18,12},{20,14},{22,8},{24,18},... | collective-permute-start | bytes 296 | tf_op jit(solution)/shard_map/ppermute | solution.py:206
  6.5 1.6 %collective-permute-start.3 = (s32[32]{0:T(128)}, s32[32]{0:T(128)S(1)}, u32[]{:S(2)}, u32[]{:S(2)}) collective-permute-start(s32[32]{0:T(128)} %bitcast.36), channel_id=1, source_target_pairs={{0,2},{2,4},{4,6},{6,0},{1,3},{3,5},{5,7},{7,1},{8,10},{10,12},{12... | collective-permute-start | bytes 392 | tf_op jit(solution)/shard_map/ppermute | solution.py:207
  8.1 1.1 %collective-permute-start.2 = (s32[1]{0:T(128)}, s32[1]{0:T(128)}, u32[]{:S(2)}, u32[]{:S(2)}) collective-permute-start(s32[1]{0:T(128)} %bitcast.1), channel_id=1, source_target_pairs={{8,2},{10,4},{12,6},{14,0},{16,10},{18,12},{20,14},{22,8},{24,18},... | collective-permute-start | bytes 20 | tf_op jit(solution)/shard_map/ppermute | solution.py:206
  10.5 0.0 copy-start
  10.5 0.6 %copy-done = s32[1,1,1,80]{3,2,1,0:T(1,128)S(1)} copy-done((s32[1,1,1,80]{3,2,1,0:T(1,128)S(1)}, s32[1,1,1,80]{3,2,1,0:T(1,128)}, u32[]{:S(2)}) %copy-start) | copy-done | bytes 344
  11.1 0.0 copy-start.1
  11.1 0.7 %copy-done.1 = s32[1,1,1,24]{3,2,1,0:T(1,128)S(1)} copy-done((s32[1,1,1,24]{3,2,1,0:T(1,128)S(1)}, s32[1,1,1,24]{3,2,1,0:T(1,128)}, u32[]{:S(2)}) %copy-start.1) | copy-done | bytes 120
  11.8 0.0 copy-start.2
  11.8 0.7 %copy-done.2 = s32[1,1,32]{2,1,0:T(1,128)S(1)} copy-done((s32[1,1,32]{2,1,0:T(1,128)S(1)}, s32[1,1,32]{2,1,0:T(1,128)}, u32[]{:S(2)}) %copy-start.2) | copy-done | bytes 152
  12.5 5.8 %first_product.1 = (f32[2,2048,128]{2,1,0:T(8,128)S(1)}, bf16[32,1024,128]{2,1,0:T(8,128)(2,1)S(1)}) custom-call(s32[24]{0:T(128)S(1)} %bitcast.35, s32[1]{0:T(128)} %bitcast.31.a_count, s32[80]{0:T(128)S(1)} %bitcast.33, s32[1]{0:T(128)} %bitcast.32.b_count, s32[32]{0:T(128)S(1)} %bitcast.37, s32[1]{0:T(128)} %bitcast.5.rot, ...), custom_call_target="tpu_custom_call" | custom-call | flops 1073741824 | bytes 12582912 | tf_op jit(solution)/shard_map/first_product/pallas_call | solution.py:132
  18.3 5.6 %collective-permute-done.2.a_count = s32[1]{0:T(128)} collective-permute-done((s32[1]{0:T(128)}, s32[1]{0:T(128)}, u32[]{:S(2)}, u32[]{:S(2)}) %collective-permute-start.2) | collective-permute-done | bytes 36 | tf_op jit(solution)/shard_map/ppermute | solution.py:206
  23.9 0.0 collective-permute-done.1.a_cells
  23.9 0.8 %collective-permute-done.3.kept = s32[32]{0:T(128)S(1)} collective-permute-done((s32[32]{0:T(128)}, s32[32]{0:T(128)S(1)}, u32[]{:S(2)}, u32[]{:S(2)}) %collective-permute-start.3) | collective-permute-done | bytes 160 | tf_op jit(solution)/shard_map/ppermute | solution.py:207
  24.7 0.0 collective-permute-done.4.a_blocks
  24.7 3.6 %second_product.1 = f32[2,2064,128]{2,1,0:T(8,128)S(1)} custom-call(s32[24]{0:T(128)S(1)} %collective-permute-done.1.a_cells, s32[1]{0:T(128)} %collective-permute-done.2.a_count, s32[32]{0:T(128)S(1)} %collective-permute-done.3.kept, s32[1]{0:T(128)} %bitcast.5.rot, bf16[24,128,128]{2,1,0:T(8,128)(2,1)S(1)} %collective-permute-done.4.a_blocks, ...), custom_call_target="tpu_custom_call" | custom-call | flops 1073741824 | bytes 8388608 | tf_op jit(solution)/shard_map/second_product/pallas_call | solution.py:152
  28.3 0.1 slice_bitcast_fusion
  28.3 0.1 collective-permute-start.5
  28.4 0.1 slice_bitcast_fusion.3
  28.5 0.6 %collective-permute-start = (f32[2048,128]{1,0:T(8,128)S(1)}, f32[2048,128]{1,0:T(8,128)S(1)}, u32[]{:S(2)}, u32[]{:S(2)}) collective-permute-start(f32[2048,128]{1,0:T(8,128)S(1)} %slice_bitcast_fusion.3), channel_id=1, source_target_pairs={{0,1},{1,0},{2,3},{3,2},{4,5},{5,4},{6,7},{7,6},{8,9},{9,8},{10,11... | collective-permute-start | bytes 3145736 | tf_op jit(solution)/shard_map/ppermute | solution.py:172
  29.0 2.0 %collective-permute-done.5 = f32[2064,128]{1,0:T(8,128)S(1)} collective-permute-done((f32[2064,128]{1,0:T(8,128)S(1)}, f32[2064,128]{1,0:T(8,128)S(1)}, u32[]{:S(2)}, u32[]{:S(2)}) %collective-permute-start.5) | collective-permute-done | bytes 1056800 | tf_op jit(solution)/shard_map/ppermute | solution.py:172
  31.1 0.1 fusion
  31.2 0.1 fusion.3
  31.4 0.1 maximum_bitcast_fusion
  31.5 1.9 %collective-permute-start.6 = (f16[2064,128]{1,0:T(8,128)(2,1)S(1)}, f16[2064,128]{1,0:T(8,128)(2,1)S(1)}, u32[]{:S(2)}, u32[]{:S(2)}) collective-permute-start(f16[2064,128]{1,0:T(8,128)(2,1)S(1)} %maximum_bitcast_fusion), channel_id=1, source_target_pairs={{0,6},{2,0},{4,2},{6,4},{1,7},{3,1},{5,3},{7,5},{8,14},{10,8},{12,... | collective-permute-start | bytes 1585160 | tf_op jit(solution)/shard_map/ppermute | solution.py:221
  33.4 12.3 %collective-permute-done.6 = f16[2064,128]{1,0:T(8,128)(2,1)S(1)} collective-permute-done((f16[2064,128]{1,0:T(8,128)(2,1)S(1)}, f16[2064,128]{1,0:T(8,128)(2,1)S(1)}, u32[]{:S(2)}, u32[]{:S(2)}) %collective-permute-start.6) | collective-permute-done | bytes 528416 | tf_op jit(solution)/shard_map/ppermute | solution.py:221
  45.6 0.1 convert_element_type.9
  45.7 0.0 collective-permute-done
  45.7 1.1 %fusion.1 = f32[2048,128]{1,0:T(8,128)} fusion(f32[2064,128]{1,0:T(8,128)S(1)} %convert_element_type.9, f32[2048,128]{1,0:T(8,128)S(1)} %collective-permute-done, f32[2,2048,128]{2,1,0:T(8,128)S(1)} %get-tuple-element.7, f32[8,128]{1,0:T(8,128)S(1)} %fusion.5), kind=kLoop, calls=%fused_computation.4 | loop fusion | flops 786432 | bytes 4198400 | tf_op jit(solution)/shard_map/add | solution.py:223
  (3 shorter events, 0.0 us)
Async XLA Ops:
  0.0 24.7 %collective-permute-start.4 = (bf16[24,128,128]{2,1,0:T(8,128)(2,1)}, bf16[24,128,128]{2,1,0:T(8,128)(2,1)S(1)}, u32[]{:S(2)}, u32[]{:S(2)}) collective-permute-start(bf16[24,128,128]{2,1,0:T(8,128)(2,1)} %bitcast.39), channel_id=1, source_target_pairs={{8,2},{10,4},{12,6},{14,0},{16,10},{18,12},{20,14},{22,8},{24,18},... | collective-permute-start | bytes 2359304 | tf_op jit(solution)/shard_map/ppermute | solution.py:205
  4.9 18.9 %collective-permute-start.1 = (s32[24]{0:T(128)}, s32[24]{0:T(128)S(1)}, u32[]{:S(2)}, u32[]{:S(2)}) collective-permute-start(s32[24]{0:T(128)} %bitcast.34), channel_id=1, source_target_pairs={{8,2},{10,4},{12,6},{14,0},{16,10},{18,12},{20,14},{22,8},{24,18},... | collective-permute-start | bytes 296 | tf_op jit(solution)/shard_map/ppermute | solution.py:206
  6.5 18.2 %collective-permute-start.3 = (s32[32]{0:T(128)}, s32[32]{0:T(128)S(1)}, u32[]{:S(2)}, u32[]{:S(2)}) collective-permute-start(s32[32]{0:T(128)} %bitcast.36), channel_id=1, source_target_pairs={{0,2},{2,4},{4,6},{6,0},{1,3},{3,5},{5,7},{7,1},{8,10},{10,12},{12... | collective-permute-start | bytes 392 | tf_op jit(solution)/shard_map/ppermute | solution.py:207
  8.1 15.8 %collective-permute-start.2 = (s32[1]{0:T(128)}, s32[1]{0:T(128)}, u32[]{:S(2)}, u32[]{:S(2)}) collective-permute-start(s32[1]{0:T(128)} %bitcast.1), channel_id=1, source_target_pairs={{8,2},{10,4},{12,6},{14,0},{16,10},{18,12},{20,14},{22,8},{24,18},... | collective-permute-start | bytes 20 | tf_op jit(solution)/shard_map/ppermute | solution.py:206
  10.5 0.7 %copy-start = (s32[1,1,1,80]{3,2,1,0:T(1,128)S(1)}, s32[1,1,1,80]{3,2,1,0:T(1,128)}, u32[]{:S(2)}) copy-start(s32[1,1,1,80]{3,2,1,0:T(1,128)} %param.11) | copy-start | bytes 964
  11.1 0.7 %copy-start.1 = (s32[1,1,1,24]{3,2,1,0:T(1,128)S(1)}, s32[1,1,1,24]{3,2,1,0:T(1,128)}, u32[]{:S(2)}) copy-start(s32[1,1,1,24]{3,2,1,0:T(1,128)} %param.8) | copy-start | bytes 292
  11.8 0.7 %copy-start.2 = (s32[1,1,32]{2,1,0:T(1,128)S(1)}, s32[1,1,32]{2,1,0:T(1,128)}, u32[]{:S(2)}) copy-start(s32[1,1,32]{2,1,0:T(1,128)} %param.13) | copy-start | bytes 388
  28.3 2.7 %collective-permute-start.5 = (f32[2064,128]{1,0:T(8,128)S(1)}, f32[2064,128]{1,0:T(8,128)S(1)}, u32[]{:S(2)}, u32[]{:S(2)}) collective-permute-start(f32[2064,128]{1,0:T(8,128)S(1)} %slice_bitcast_fusion), channel_id=1, source_target_pairs={{0,1},{1,0},{2,3},{3,2},{4,5},{5,4},{6,7},{7,6},{8,9},{9,8},{10,11... | collective-permute-start | bytes 3170312 | tf_op jit(solution)/shard_map/ppermute | solution.py:172
  28.5 17.2 %collective-permute-start = (f32[2048,128]{1,0:T(8,128)S(1)}, f32[2048,128]{1,0:T(8,128)S(1)}, u32[]{:S(2)}, u32[]{:S(2)}) collective-permute-start(f32[2048,128]{1,0:T(8,128)S(1)} %slice_bitcast_fusion.3), channel_id=1, source_target_pairs={{0,1},{1,0},{2,3},{3,2},{4,5},{5,4},{6,7},{7,6},{8,9},{9,8},{10,11... | collective-permute-start | bytes 3145736 | tf_op jit(solution)/shard_map/ppermute | solution.py:172
  31.5 14.1 %collective-permute-start.6 = (f16[2064,128]{1,0:T(8,128)(2,1)S(1)}, f16[2064,128]{1,0:T(8,128)(2,1)S(1)}, u32[]{:S(2)}, u32[]{:S(2)}) collective-permute-start(f16[2064,128]{1,0:T(8,128)(2,1)S(1)} %maximum_bitcast_fusion), channel_id=1, source_target_pairs={{0,6},{2,0},{4,2},{6,4},{1,7},{3,1},{5,3},{7,5},{8,14},{10,8},{12,... | collective-permute-start | bytes 1585160 | tf_op jit(solution)/shard_map/ppermute | solution.py:221

commit v6 on v5

--- a/solution.py
+++ b/solution.py
@@ -36,12 +36,12 @@
         pltpu.make_async_copy(blocks.at[slot], cell_ref(cell), sem).start()
 
 
-def pair_up(kept, first, second, pending):
+def pair_up(kept, rot, places, first, second, pending):
     for row in range(CR):
         pending[row] = -1
     count = 0
-    for place in range(kept.shape[0]):
-        row = kept[place] // CC
+    for place in places:
+        row = kept_cell(kept, rot, place) // CC
         waiting = pending[row]
         first[count], second[count] = waiting, place
         count = count + (waiting >= 0).astype(jnp.int32)
@@ -50,35 +50,45 @@
         waiting = pending[row]
         first[count], second[count] = waiting, waiting
         count = count + (waiting >= 0).astype(jnp.int32)
-    for spare in range(CR // 2):
+    for spare in range(most_pairs(len(places)) - pl.cdiv(len(places), 2)):
         first[count + spare], second[count + spare] = first[0], second[0]
 
 
-def pairs_of(capacity):
-    return (capacity + CR) // 2
-
-
-def multiply_kept(kept, rot, first, second, left, right, out, bs):
-    total, layers = kept.shape[0], out.shape[0]
-    share = total // layers
+def most_pairs(places):
+    return (places + CR) // 2
+
+
+def kept_cell(kept, rot, place):
+    return kept[lax.rem(place + rot[0], kept.shape[0])]
+
+
+def multiply_kept(kept, rot, places, lists, left, right, out, bs):
+    first, second, pending = lists
+    share = len(places) // out.shape[0]
+    pair_up(kept, rot, places, first, second, pending)
     top = jnp.zeros((8, bs), jnp.float32)
-    for pair in range(pairs_of(total)):
-        places = first[pair], second[pair]
-        cells = [kept[place] for place in places]
+    for pair in range(most_pairs(len(places))):
+        chosen = first[pair], second[pair]
+        cells = [kept_cell(kept, rot, place) for place in chosen]
         rows = left[pl.ds(pl.multiple_of((cells[0] // CC) * bs, bs), bs)]
         cols = jnp.concatenate([right[cell % CC] for cell in cells], axis=1)
         product = jnp.dot(rows, cols, preferred_element_type=jnp.float32)
-        for half, place in enumerate(places):
+        for half, place in enumerate(chosen):
             block = product[:, half * bs : (half + 1) * bs]
-            to = lax.rem(place - rot[0] + total, total)
-            start = pl.multiple_of((to % share) * bs, bs)
-            out[to // share, pl.ds(start, bs)] = block
+            to = place - places[0]
+            out[to // share, pl.ds(pl.multiple_of((to % share) * bs, bs), bs)] = block
             top = jnp.maximum(top, jnp.max(jnp.abs(block).reshape(-1, 8, bs), axis=0))
     return top
 
 
+def put_notes(out, top):
+    for part in range(out.shape[0]):
+        for start in range(out.shape[1] - NOTE_ROWS, out.shape[1], 8):
+            out[part, start : start + 8] = top
+
+
 def first_kernel(bs, a_cells, a_count, b_cells, b_count, kept, rot, a_blocks, b_blocks, *refs):
-    out, dense, left, first, second, pending, a_sem, b_sem = refs
+    out, dense, left, *lists, a_sem, b_sem = refs
 
     @pl.loop(0, CC)
     def _(col):
@@ -89,14 +99,13 @@
         b_blocks, b_cells, b_count, KW * CC, lambda cell: right_cell(dense, cell, bs), b_sem
     )
     place_slots(a_blocks, a_cells, a_count, CR * KW, lambda cell: left_cell(left, cell, bs), a_sem)
-    pair_up(kept, first, second, pending)
     pltpu.make_async_copy(b_blocks, b_blocks, b_sem).wait()
     pltpu.make_async_copy(a_blocks, a_blocks, a_sem).wait()
-    multiply_kept(kept, rot, first, second, left, dense, out, bs)
-
-
-def second_kernel(bs, a_cells, a_count, kept, rot, a_blocks, dense, *refs):
-    out, left, a_slot, first, second, pending = refs
+    multiply_kept(kept, rot, range(kept.shape[0]), lists, left, dense, out, bs)
+
+
+def others_kernel(bs, a_cells, a_count, kept, rot, a_blocks, dense, *refs):
+    out, left, a_slot, *lists = refs
     for cell in range(CR * KW):
         a_slot[cell] = -1
 
@@ -104,25 +113,28 @@
     def _(slot):
         a_slot[a_cells[slot]] = slot
 
-    pair_up(kept, first, second, pending)
     for cell in range(CR * KW):
         slot = a_slot[cell]
         block = a_blocks[jnp.maximum(slot, 0)]
         left_cell(left, cell, bs)[...] = jnp.where(slot >= 0, block, jnp.zeros_like(block))
 
-    top = multiply_kept(kept, rot, first, second, left, dense, out, bs)
-    for layer in range(out.shape[0]):
-        for start in range(out.shape[1] - NOTE_ROWS, out.shape[1], 8):
-            out[layer, start : start + 8] = top
+    places = range(kept.shape[0] // (out.shape[0] + 1), kept.shape[0])
+    put_notes(out, multiply_kept(kept, rot, places, lists, left, dense, out, bs))
+
+
+def own_kernel(bs, kept, rot, left, dense, *refs):
+    out, *lists = refs
+    places = range((out.shape[1] - NOTE_ROWS) // bs)
+    put_notes(out, multiply_kept(kept, rot, places, lists, left, dense, out, bs))
 
 
 def cost(bytes_accessed, bs):
-    flops = CR * KW * CC * bs**3
+    flops = CR * KW * CC * bs**3 // 2
     return pl.CostEstimate(flops=flops, bytes_accessed=bytes_accessed, transcendentals=0)
 
 
-def pair_scratch(capacity):
-    lists = pltpu.SMEM((pairs_of(capacity) + CR // 2,), jnp.int32)
+def pair_lists(places):
+    lists = pltpu.SMEM((most_pairs(places) + CR // 2,), jnp.int32)
     return [lists, lists, pltpu.SMEM((CR,), jnp.int32)]
 
 
@@ -139,38 +151,50 @@
         in_specs=[SMEM] * 6 + [HBM] * 2,
         out_specs=[VMEM] * 2,
         scratch_shapes=[pltpu.VMEM(((CR + spare_a) * bs, KW * bs), a_blocks.dtype)]
-        + pair_scratch(kept.shape[0])
+        + pair_lists(kept.shape[0])
         + [pltpu.SemaphoreType.DMA] * 2,
         compiler_params=pltpu.CompilerParams(vmem_limit_bytes=20 << 20),
         cost_estimate=cost(12 << 20, bs),
     )(a_cells, a_count, b_cells, b_count, kept, rot, a_blocks, b_blocks)
 
 
-def run_second(layers, a_cells, a_count, kept, rot, a_blocks, dense):
-    bs = a_blocks.shape[-1]
-    rows = kept.shape[0] // layers * bs + NOTE_ROWS
+def run_others(layers, a_cells, a_count, kept, rot, a_blocks, dense):
+    bs, share = a_blocks.shape[-1], kept.shape[0] // layers
     return pl.pallas_call(
-        functools.partial(second_kernel, bs),
-        name="second_product",
-        out_shape=jax.ShapeDtypeStruct((layers, rows, bs), jnp.float32),
+        functools.partial(others_kernel, bs),
+        name="others_product",
+        out_shape=[
+            jax.ShapeDtypeStruct((layers - 1, share * bs + NOTE_ROWS, bs), jnp.float32),
+            jax.ShapeDtypeStruct((CR * bs, KW * bs), a_blocks.dtype),
+        ],
         in_specs=[SMEM] * 4 + [VMEM] * 2,
-        out_specs=VMEM,
-        scratch_shapes=[
-            pltpu.VMEM((CR * bs, KW * bs), a_blocks.dtype),
-            pltpu.SMEM((CR * KW,), jnp.int32),
-        ]
-        + pair_scratch(kept.shape[0]),
+        out_specs=[VMEM] * 2,
+        scratch_shapes=[pltpu.SMEM((CR * KW,), jnp.int32)] + pair_lists(kept.shape[0] - share),
         compiler_params=pltpu.CompilerParams(vmem_limit_bytes=20 << 20),
         cost_estimate=cost(8 << 20, bs),
     )(a_cells, a_count, kept, rot, a_blocks, dense)
 
 
-def over_layers(combine, values, layers):
-    total = values[0]
+def run_own(layers, kept, rot, left, dense):
+    bs, share = dense.shape[-1], kept.shape[0] // layers
+    return pl.pallas_call(
+        functools.partial(own_kernel, bs),
+        name="own_product",
+        out_shape=jax.ShapeDtypeStruct((1, share * bs + NOTE_ROWS, bs), jnp.float32),
+        in_specs=[SMEM] * 2 + [VMEM] * 2,
+        out_specs=VMEM,
+        scratch_shapes=pair_lists(share),
+        compiler_params=pltpu.CompilerParams(vmem_limit_bytes=20 << 20),
+        cost_estimate=cost(8 << 20, bs),
+    )(kept, rot, left, dense)
+
+
+def from_layers(parts, layers):
+    gained = []
     for step in range(1, layers):
         perm = [(i, (i + step) % layers) for i in range(layers)]
-        total = combine(total, lax.ppermute(values[step], "layer", perm))
-    return total
+        gained.append(lax.ppermute(parts[step - 1], "layer", perm))
+    return gained
 
 
 def narrow(value):
@@ -216,10 +240,13 @@
         pltpu.with_memory_space_constraint(a_blocks, pltpu.HBM),
         pltpu.with_memory_space_constraint(b_blocks, pltpu.HBM),
     )
-    second = run_second(layers, moved_cells, moved_count, moved_kept, rot, moved_blocks, dense)
-    other = over_layers(jnp.add, second, layers)
-    back = lax.ppermute(narrow(other), "col", to_last)
-    own = over_layers(jnp.add, first, layers)
+    others, left = run_others(
+        layers, moved_cells, moved_count, moved_kept, rot, moved_blocks, dense
+    )
+    gained = from_layers(others, layers)
+    own = run_own(layers, moved_kept, rot, left, dense)[0]
+    back = lax.ppermute(narrow(sum(gained, own)), "col", to_last)
+    own = sum(from_layers(first[1:], layers), first[0])
     total = own + widen(back)
     return total.reshape(1, 1, share, bs, bs)
 

time: 47.1 us -> 46.3 us (0.983)
  waiting for transfers between devices: 20.7 us -> 18.9 us
  Pallas kernels: 9.36 us -> 10.5 us
    ppermute x3, waiting for transfers between devices: 14.3 us -> 12.5 us  [the longest x1 12.3 us: on_device(): back = lax.ppermute(narrow(sum(gained, own)), 'col', to_last)]
    pallas_call x1 -> x2, Pallas kernels: 3.57 us -> 4.64 us  [the longest x1 2.88 us: run_others(): pl.pallas_call(functools.partial(others_kernel, bs), name='others_product...]
  transfers between devices with their start and end apart: 7 -> 7, of which waited for: 4 -> 4; matrix products, arithmetic and copies ran while one was open for 1% -> 1% of each run, Pallas kernels for 12% -> 17%
where the time goes in v6:
time: 46.3 us; the launch traced here: 46 us
  waiting for transfers between devices  18.9 us (41%)
  starting transfers between devices  11.6 us (25%)
  Pallas kernels  10.5 us (23%)
  local copies, waits for them, and re-layouts  2.03 us (4%)
  other arithmetic  1.57 us (3%)
  between operations  1.44 us (3%)
    ppermute x1, waiting for transfers between devices, on_device(): back = lax.ppermute(narrow(sum(gained, own)), 'col', to_last)  12.3 us
    pallas_call x1, Pallas kernels, run_first(): pl.pallas_call(functools.partial(first_kernel, bs), name='first_product',...  5.85 us
    ppermute x2, waiting for transfers between devices, on_device(): lax.ppermute((a_cells, a_count), ('row', 'col'), to_b)  5.67 us
    ppermute x1, starting transfers between devices, on_device(): moved_blocks = lax.ppermute(a_blocks, ('row', 'col'), to_b)  4.94 us
    pallas_call x1, Pallas kernels, run_others(): pl.pallas_call(functools.partial(others_kernel, bs), name='others_product...  2.88 us
    ppermute x2, starting transfers between devices, on_device(): lax.ppermute((a_cells, a_count), ('row', 'col'), to_b)  2.64 us
    unnamed x6, local copies, waits for them, and re-layouts  1.96 us
    ppermute x1, starting transfers between devices, on_device(): back = lax.ppermute(narrow(sum(gained, own)), 'col', to_last)  1.85 us
  transfers between devices with their start and end apart: 7, of which 4 were waited for; matrix products, arithmetic and copies ran while one was open for 1% of the time, Pallas kernels for 17%

profile of v6, /device:TPU:0, one launch (start us, length us, event | category | flops | bytes accessed | tf_op | source)
XLA Modules:
  0.0 46.0 jit_solution(13828450797287201156)
XLA Ops:
  0.0 4.9 %collective-permute-start.4 = (bf16[24,128,128]{2,1,0:T(8,128)(2,1)}, bf16[24,128,128]{2,1,0:T(8,128)(2,1)S(1)}, u32[]{:S(2)}, u32[]{:S(2)}) collective-permute-start(bf16[24,128,128]{2,1,0:T(8,128)(2,1)} %bitcast.37), channel_id=1, source_target_pairs={{8,2},{10,4},{12,6},{14,0},{16,10},{18,12},{20,14},{22,8},{24,18},... | collective-permute-start | bytes 2359304 | tf_op jit(solution)/shard_map/ppermute | solution.py:229
  4.9 1.6 %collective-permute-start.1 = (s32[32]{0:T(128)}, s32[32]{0:T(128)S(1)}, u32[]{:S(2)}, u32[]{:S(2)}) collective-permute-start(s32[32]{0:T(128)} %bitcast.33), channel_id=1, source_target_pairs={{0,2},{2,4},{4,6},{6,0},{1,3},{3,5},{5,7},{7,1},{8,10},{10,12},{12... | collective-permute-start | bytes 392 | tf_op jit(solution)/shard_map/ppermute | solution.py:231
  6.5 1.5 %collective-permute-start.2 = (s32[24]{0:T(128)}, s32[24]{0:T(128)S(1)}, u32[]{:S(2)}, u32[]{:S(2)}) collective-permute-start(s32[24]{0:T(128)} %bitcast.31), channel_id=1, source_target_pairs={{8,2},{10,4},{12,6},{14,0},{16,10},{18,12},{20,14},{22,8},{24,18},... | collective-permute-start | bytes 296 | tf_op jit(solution)/shard_map/ppermute | solution.py:230
  8.1 1.1 %collective-permute-start.3 = (s32[1]{0:T(128)}, s32[1]{0:T(128)}, u32[]{:S(2)}, u32[]{:S(2)}) collective-permute-start(s32[1]{0:T(128)} %bitcast.1), channel_id=1, source_target_pairs={{8,2},{10,4},{12,6},{14,0},{16,10},{18,12},{20,14},{22,8},{24,18},... | collective-permute-start | bytes 20 | tf_op jit(solution)/shard_map/ppermute | solution.py:230
  10.5 0.0 copy-start
  10.5 0.6 %copy-done = s32[1,1,1,80]{3,2,1,0:T(1,128)S(1)} copy-done((s32[1,1,1,80]{3,2,1,0:T(1,128)S(1)}, s32[1,1,1,80]{3,2,1,0:T(1,128)}, u32[]{:S(2)}) %copy-start) | copy-done | bytes 344
  11.1 0.0 copy-start.1
  11.1 0.7 %copy-done.1 = s32[1,1,1,24]{3,2,1,0:T(1,128)S(1)} copy-done((s32[1,1,1,24]{3,2,1,0:T(1,128)S(1)}, s32[1,1,1,24]{3,2,1,0:T(1,128)}, u32[]{:S(2)}) %copy-start.1) | copy-done | bytes 120
  11.8 0.0 copy-start.2
  11.8 0.7 %copy-done.2 = s32[1,1,32]{2,1,0:T(1,128)S(1)} copy-done((s32[1,1,32]{2,1,0:T(1,128)S(1)}, s32[1,1,32]{2,1,0:T(1,128)}, u32[]{:S(2)}) %copy-start.2) | copy-done | bytes 152
  12.5 5.8 %first_product.1 = (f32[2,2048,128]{2,1,0:T(8,128)S(1)}, bf16[32,1024,128]{2,1,0:T(8,128)(2,1)S(1)}) custom-call(s32[24]{0:T(128)S(1)} %bitcast.32, s32[1]{0:T(128)} %bitcast.28.a_count, s32[80]{0:T(128)S(1)} %bitcast.30, s32[1]{0:T(128)} %bitcast.29.b_count, s32[32]{0:T(128)S(1)} %bitcast.34, s32[1]{0:T(128)} %bitcast.5.rot, ...), custom_call_target="tpu_custom_call" | custom-call | flops 536870912 | bytes 12582912 | tf_op jit(solution)/shard_map/first_product/pallas_call | solution.py:144
  18.3 5.7 %collective-permute-done.3.a_count = s32[1]{0:T(128)} collective-permute-done((s32[1]{0:T(128)}, s32[1]{0:T(128)}, u32[]{:S(2)}, u32[]{:S(2)}) %collective-permute-start.3) | collective-permute-done | bytes 36 | tf_op jit(solution)/shard_map/ppermute | solution.py:230
  24.0 0.0 collective-permute-done.2.a_cells
  24.0 0.7 %collective-permute-done.1.kept = s32[32]{0:T(128)S(1)} collective-permute-done((s32[32]{0:T(128)}, s32[32]{0:T(128)S(1)}, u32[]{:S(2)}, u32[]{:S(2)}) %collective-permute-start.1) | collective-permute-done | bytes 160 | tf_op jit(solution)/shard_map/ppermute | solution.py:231
  24.7 0.0 collective-permute-done.4.a_blocks
  24.7 2.9 %others_product.1 = (f32[1,2064,128]{2,1,0:T(8,128)S(1)}, bf16[512,1024]{1,0:T(8,128)(2,1)S(1)}) custom-call(s32[24]{0:T(128)S(1)} %collective-permute-done.2.a_cells, s32[1]{0:T(128)} %collective-permute-done.3.a_count, s32[32]{0:T(128)S(1)} %collective-permute-done.1.kept, s32[1]{0:T(128)} %bitcast.5.rot, ...), custom_call_target="tpu_custom_call" | custom-call | flops 536870912 | bytes 8388608 | tf_op jit(solution)/shard_map/others_product/pallas_call | solution.py:163
  27.6 0.1 collective-permute-start.5
  27.6 0.1 slice_bitcast_fusion.1
  27.7 0.6 %collective-permute-start = (f32[2048,128]{1,0:T(8,128)S(1)}, f32[2048,128]{1,0:T(8,128)S(1)}, u32[]{:S(2)}, u32[]{:S(2)}) collective-permute-start(f32[2048,128]{1,0:T(8,128)S(1)} %slice_bitcast_fusion.1), channel_id=1, source_target_pairs={{0,1},{1,0},{2,3},{3,2},{4,5},{5,4},{6,7},{7,6},{8,9},{9,8},{10,11... | collective-permute-start | bytes 3145736 | tf_op jit(solution)/shard_map/ppermute | solution.py:196
  28.3 1.8 %own_product.1 = f32[1,2064,128]{2,1,0:T(8,128)S(1)} custom-call(s32[32]{0:T(128)S(1)} %collective-permute-done.1.kept, s32[1]{0:T(128)} %bitcast.5.rot, bf16[512,1024]{1,0:T(8,128)(2,1)S(1)} %get-tuple-element.11.left, bf16[32,1024,128]{2,1,0:T(8,128)(2,1)S(1)} %get-tuple-element.10.dense), custom_call_target="tpu_custom_call" | custom-call | flops 536870912 | bytes 8388608 | tf_op jit(solution)/shard_map/own_product/pallas_call | solution.py:180
  30.0 0.3 collective-permute-done.5
  30.3 0.1 bitcast_add_fusion
  30.4 0.1 fusion.2
  30.6 0.1 maximum_bitcast_fusion
  30.7 1.8 %collective-permute-start.6 = (f16[2064,128]{1,0:T(8,128)(2,1)S(1)}, f16[2064,128]{1,0:T(8,128)(2,1)S(1)}, u32[]{:S(2)}, u32[]{:S(2)}) collective-permute-start(f16[2064,128]{1,0:T(8,128)(2,1)S(1)} %maximum_bitcast_fusion), channel_id=1, source_target_pairs={{0,6},{2,0},{4,2},{6,4},{1,7},{3,1},{5,3},{7,5},{8,14},{10,8},{12,... | collective-permute-start | bytes 1585160 | tf_op jit(solution)/shard_map/ppermute | solution.py:248
  32.6 12.3 %collective-permute-done.6 = f16[2064,128]{1,0:T(8,128)(2,1)S(1)} collective-permute-done((f16[2064,128]{1,0:T(8,128)(2,1)S(1)}, f16[2064,128]{1,0:T(8,128)(2,1)S(1)}, u32[]{:S(2)}, u32[]{:S(2)}) %collective-permute-start.6) | collective-permute-done | bytes 528416 | tf_op jit(solution)/shard_map/ppermute | solution.py:248
  44.8 0.1 convert_element_type.9
  44.9 0.0 collective-permute-done
  44.9 1.1 %fusion = f32[2048,128]{1,0:T(8,128)} fusion(f32[2064,128]{1,0:T(8,128)S(1)} %convert_element_type.9, f32[2048,128]{1,0:T(8,128)S(1)} %collective-permute-done, f32[2,2048,128]{2,1,0:T(8,128)S(1)} %get-tuple-element.9, f32[8,128]{1,0:T(8,128)S(1)} %fusion.4), kind=kLoop, calls=%fused_computation.2 | loop fusion | flops 786432 | bytes 4198400 | tf_op jit(solution)/shard_map/add | solution.py:250
  (3 shorter events, 0.0 us)
Async XLA Ops:
  0.0 24.7 %collective-permute-start.4 = (bf16[24,128,128]{2,1,0:T(8,128)(2,1)}, bf16[24,128,128]{2,1,0:T(8,128)(2,1)S(1)}, u32[]{:S(2)}, u32[]{:S(2)}) collective-permute-start(bf16[24,128,128]{2,1,0:T(8,128)(2,1)} %bitcast.37), channel_id=1, source_target_pairs={{8,2},{10,4},{12,6},{14,0},{16,10},{18,12},{20,14},{22,8},{24,18},... | collective-permute-start | bytes 2359304 | tf_op jit(solution)/shard_map/ppermute | solution.py:229
  4.9 19.7 %collective-permute-start.1 = (s32[32]{0:T(128)}, s32[32]{0:T(128)S(1)}, u32[]{:S(2)}, u32[]{:S(2)}) collective-permute-start(s32[32]{0:T(128)} %bitcast.33), channel_id=1, source_target_pairs={{0,2},{2,4},{4,6},{6,0},{1,3},{3,5},{5,7},{7,1},{8,10},{10,12},{12... | collective-permute-start | bytes 392 | tf_op jit(solution)/shard_map/ppermute | solution.py:231
  6.5 17.5 %collective-permute-start.2 = (s32[24]{0:T(128)}, s32[24]{0:T(128)S(1)}, u32[]{:S(2)}, u32[]{:S(2)}) collective-permute-start(s32[24]{0:T(128)} %bitcast.31), channel_id=1, source_target_pairs={{8,2},{10,4},{12,6},{14,0},{16,10},{18,12},{20,14},{22,8},{24,18},... | collective-permute-start | bytes 296 | tf_op jit(solution)/shard_map/ppermute | solution.py:230
  8.1 15.9 %collective-permute-start.3 = (s32[1]{0:T(128)}, s32[1]{0:T(128)}, u32[]{:S(2)}, u32[]{:S(2)}) collective-permute-start(s32[1]{0:T(128)} %bitcast.1), channel_id=1, source_target_pairs={{8,2},{10,4},{12,6},{14,0},{16,10},{18,12},{20,14},{22,8},{24,18},... | collective-permute-start | bytes 20 | tf_op jit(solution)/shard_map/ppermute | solution.py:230
  10.5 0.7 %copy-start = (s32[1,1,1,80]{3,2,1,0:T(1,128)S(1)}, s32[1,1,1,80]{3,2,1,0:T(1,128)}, u32[]{:S(2)}) copy-start(s32[1,1,1,80]{3,2,1,0:T(1,128)} %param.11) | copy-start | bytes 964
  11.1 0.7 %copy-start.1 = (s32[1,1,1,24]{3,2,1,0:T(1,128)S(1)}, s32[1,1,1,24]{3,2,1,0:T(1,128)}, u32[]{:S(2)}) copy-start(s32[1,1,1,24]{3,2,1,0:T(1,128)} %param.8) | copy-start | bytes 292
  11.8 0.7 %copy-start.2 = (s32[1,1,32]{2,1,0:T(1,128)S(1)}, s32[1,1,32]{2,1,0:T(1,128)}, u32[]{:S(2)}) copy-start(s32[1,1,32]{2,1,0:T(1,128)} %param.13) | copy-start | bytes 388
  27.6 2.7 %collective-permute-start.5 = (f32[2064,128]{1,0:T(8,128)S(1)}, f32[2064,128]{1,0:T(8,128)S(1)}, u32[]{:S(2)}, u32[]{:S(2)}) collective-permute-start(f32[2064,128]{1,0:T(8,128)S(1)} %bitcast.35), channel_id=1, source_target_pairs={{0,1},{1,0},{2,3},{3,2},{4,5},{5,4},{6,7},{7,6},{8,9},{9,8},{10,11... | collective-permute-start | bytes 3170312 | tf_op jit(solution)/shard_map/ppermute | solution.py:196
  27.7 17.2 %collective-permute-start = (f32[2048,128]{1,0:T(8,128)S(1)}, f32[2048,128]{1,0:T(8,128)S(1)}, u32[]{:S(2)}, u32[]{:S(2)}) collective-permute-start(f32[2048,128]{1,0:T(8,128)S(1)} %slice_bitcast_fusion.1), channel_id=1, source_target_pairs={{0,1},{1,0},{2,3},{3,2},{4,5},{5,4},{6,7},{7,6},{8,9},{9,8},{10,11... | collective-permute-start | bytes 3145736 | tf_op jit(solution)/shard_map/ppermute | solution.py:196
  30.7 14.1 %collective-permute-start.6 = (f16[2064,128]{1,0:T(8,128)(2,1)S(1)}, f16[2064,128]{1,0:T(8,128)(2,1)S(1)}, u32[]{:S(2)}, u32[]{:S(2)}) collective-permute-start(f16[2064,128]{1,0:T(8,128)(2,1)S(1)} %maximum_bitcast_fusion), channel_id=1, source_target_pairs={{0,6},{2,0},{4,2},{6,4},{1,7},{3,1},{5,3},{7,5},{8,14},{10,8},{12,... | collective-permute-start | bytes 1585160 | tf_op jit(solution)/shard_map/ppermute | solution.py:248
